TPU v7x, 128 devices: a whole 4x4x4 slice. The times are simulated.
128 devices in a mesh: seq: 32 (over y, z, core), tp: 4 (over x).
Axes of the slice: x: 4, y: 4, z: 4, core: 2. Of those that a mesh axis runs over, the one named last changes fastest.
Arguments:
- hidden_cat: bfloat16 [16384, 7168], P('seq'), may hold values from -6 to 6
- norm_gain: float32 [7168], replicated, may hold values from 0.5 to 1.5
- k_weight: bfloat16 [7168, 3584], P('seq', 'tp'), may hold values from -0.0625 to 0.0625
- v_weight: bfloat16 [7168, 3584], P('seq', 'tp'), may hold values from -0.0625 to 0.0625
- k_down: bfloat16 [7168, 128], P('seq'), may hold values from -0.0625 to 0.0625
- v_down: bfloat16 [7168, 128], P('seq'), may hold values from -0.0625 to 0.0625
- k_up: bfloat16 [128, 3584], P(None, 'tp'), may hold values from -0.23925781 to 0.23925781
- v_up: bfloat16 [128, 3584], P(None, 'tp'), may hold values from -0.23925781 to 0.23925781
- queries: bfloat16 [16384, 3584], P('seq', 'tp')
- o_weight: bfloat16 [3584, 3584], P('tp'), may hold values from -0.09375 to 0.09375
- final_gain: float32 [3584], replicated, may hold values from 0.5 to 1.5
- unembed: bfloat16 [32000, 3584], P(('seq', 'tp')), may hold values from -0.29882812 to 0.29882812
- lengths: int32 [12], replicated, may hold values from 1 to 2048, 16384 in all
- req_prompt: int32 [16], replicated, may hold values from 0 to 11
- page_owner: int32 [2048], P('seq'), may hold values from 0 to 31, as said below
Outputs:
- attended: bfloat16 [16384, 3584], P('seq', 'tp')
- kv_cache: bfloat16 [2048, 8, 2, 3584], P('seq', None, None, 'tp')
- state_norm: float32 [16], replicated
- logit_max: float32 [16], replicated
Inputs may be any that keep to these rules, and one draw needn't show every extreme that they name: `lengths`: they sum to 16384; the longest is exactly 2048. `page_owner`: within the 64 entries of each index of seq, every owner appears exactly 2 times.
All inputs are finite; a program needn't handle non-finite values.
Results may differ from a plain program's by a relative error of at most 0.007.
The roundings to bfloat16 on the way count: a program that leaves them out, or rounds other values in their place, can miss the bound.
Values may be sent and summed in bfloat16 or wider, within the bound.
A program may use at most 192 MiB of HBM per device.

v0:
```python
import jax
import jax.numpy as jnp
from jax import lax
from jax.sharding import PartitionSpec as P

HEAD = 224
PAGE = 8
LOOKBACK = 4
NPROMPT = 12


def passed_along(value, axis, steps):
    count = lax.axis_size(axis)
    leading, last = (max(0, -steps), min(count, count - steps))
    return lax.ppermute(value, axis, [(source, source + steps) for source in range(leading, last)])


def segment_of(positions, bounds):
    counted = jnp.sum((bounds[None, :] <= positions[:, None]).astype(jnp.int32), axis=1)
    return jnp.where(positions < 0, -1, counted)


def local(
    hidden_cat,
    norm_gain,
    k_weight,
    v_weight,
    k_down,
    v_down,
    k_up,
    v_up,
    queries,
    o_weight,
    final_gain,
    unembed,
    lengths,
    req_prompt,
    page_owner,
):
    rows_here = hidden_cat.shape[0]
    width = k_weight.shape[1]
    heads_here = width // HEAD
    seq_count = lax.axis_size("seq")
    wide = hidden_cat.astype(jnp.float32)
    inverse = lax.rsqrt(jnp.mean(wide * wide, axis=1, keepdims=True) + 1e-05)
    normed = (wide * inverse * norm_gain).astype(jnp.bfloat16)

    def add_pair(w_piece, d_piece):
        return (
            jnp.dot(normed, w_piece, preferred_element_type=jnp.float32),
            jnp.dot(normed, d_piece, preferred_element_type=jnp.float32),
        )

    pieces = (
        lax.all_gather(k_weight, "seq", axis=0, tiled=True),
        lax.all_gather(k_down, "seq", axis=0, tiled=True),
    )
    key_base, key_low = add_pair(pieces[0], pieces[1])
    pieces = (
        lax.all_gather(v_weight, "seq", axis=0, tiled=True),
        lax.all_gather(v_down, "seq", axis=0, tiled=True),
    )
    value_base, value_low = add_pair(pieces[0], pieces[1])
    key_rows = (
        key_base + jnp.dot(key_low.astype(jnp.bfloat16), k_up, preferred_element_type=jnp.float32)
    ).astype(jnp.bfloat16)
    value_rows = (
        value_base
        + jnp.dot(value_low.astype(jnp.bfloat16), v_up, preferred_element_type=jnp.float32)
    ).astype(jnp.bfloat16)
    local_kv = jnp.stack([key_rows, value_rows], axis=1)
    kv_blocks = [local_kv]
    for offset in range(1, LOOKBACK + 1):
        kv_blocks.append(passed_along(local_kv, "seq", offset))
    bounds = jnp.cumsum(lengths)
    first_row = lax.axis_index("seq") * rows_here
    query_pos = first_row + jnp.arange(rows_here, dtype=jnp.int32)
    query_seg = segment_of(query_pos, bounds)
    query_heads = queries.reshape(rows_here, heads_here, HEAD)
    scale = 1.0 / HEAD**0.5
    score_list = []
    value_list = []
    for offset in range(LOOKBACK + 1):
        key_block = kv_blocks[offset][:, 0].reshape(rows_here, heads_here, HEAD)
        key_pos = query_pos - offset * rows_here
        key_seg = segment_of(key_pos, bounds)
        visible = (query_seg[:, None] == key_seg[None, :]) & (
            key_pos[None, :] <= query_pos[:, None]
        )

        def compute_scores(key_block=key_block, visible=visible):
            raw = (
                jnp.einsum(
                    "qhd,khd->hqk", query_heads, key_block, preferred_element_type=jnp.float32
                )
                * scale
            )
            return jnp.where(visible[None], raw, -1e30)

        blocked = compute_scores()
        score_list.append(blocked)
        value_list.append(kv_blocks[offset][:, 1].reshape(rows_here, heads_here, HEAD))
    scores = jnp.concatenate(score_list, axis=2)
    value_all = jnp.concatenate(value_list, axis=0)
    row_max = jnp.max(scores, axis=2, keepdims=True)
    expo_terms = jnp.exp(scores - row_max)
    probs = (expo_terms / jnp.sum(expo_terms, axis=2, keepdims=True)).astype(jnp.bfloat16)
    mixed = jnp.einsum("hqk,khd->qhd", probs, value_all, preferred_element_type=jnp.float32)
    attended = mixed.reshape(rows_here, width).astype(jnp.bfloat16)
    pages_here = rows_here // PAGE
    per_owner = pages_here // seq_count
    onehot = (page_owner[:, None] == jnp.arange(seq_count, dtype=jnp.int32)[None, :]).astype(
        jnp.int32
    )
    before = jnp.cumsum(onehot, axis=0) - onehot
    earlier = jnp.sum(before * onehot, axis=1)
    target = page_owner * per_owner + earlier
    pages = local_kv.reshape(pages_here, PAGE, 2, width)
    outgoing = jnp.zeros_like(pages).at[target].set(pages)
    kv_cache = lax.all_to_all(outgoing, "seq", split_axis=0, concat_axis=0, tiled=True)
    last_pos = bounds - 1
    request_pos = jnp.sum(
        jnp.where(
            req_prompt[:, None] == jnp.arange(NPROMPT, dtype=jnp.int32)[None, :],
            last_pos[None, :],
            0,
        ),
        axis=1,
    )
    selector = (request_pos[:, None] == query_pos[None, :]).astype(jnp.bfloat16)
    picked = jnp.dot(selector, attended, preferred_element_type=jnp.float32).astype(jnp.bfloat16)
    partial_state = jnp.dot(picked, o_weight, preferred_element_type=jnp.float32)
    state = lax.psum(partial_state, ("seq", "tp"))
    state_norm = jnp.sqrt(jnp.sum(state * state, axis=1))
    final = (
        state * lax.rsqrt(jnp.mean(state * state, axis=1, keepdims=True) + 1e-05) * final_gain
    ).astype(jnp.bfloat16)
    logits = lax.dot_general(
        final, unembed, (((1,), (1,)), ((), ())), preferred_element_type=jnp.float32
    )
    logit_max = lax.pmax(jnp.max(logits, axis=1), ("seq", "tp"))
    return (attended, kv_cache, state_norm, logit_max)


def solution(mesh):
    placed = (
        P("seq", None),
        P(),
        P("seq", "tp"),
        P("seq", "tp"),
        P("seq", None),
        P("seq", None),
        P(None, "tp"),
        P(None, "tp"),
        P("seq", "tp"),
        P("tp", None),
        P(),
        P(("seq", "tp"), None),
        P(),
        P(),
        P("seq"),
    )
    return jax.shard_map(
        local,
        mesh=mesh,
        in_specs=placed,
        out_specs=(P("seq", "tp"), P("seq", None, None, "tp"), P(), P()),
        check_vma=False,
    )
```

profile of v0, /device:TPU:1, one launch (start us, length us, event | category | flops | bytes accessed | tf_op | source)
XLA Modules:
  0.0 740.0 jit_solution(17328747703807944115)
XLA Ops:
  13.4 4.6 fusion.1
  18.0 39.3 %all-gather.11.cloned.1.call-done = bf16[7168,128]{1,0:T(8,128)(2,1)} async-done(((bf16[224,128]{1,0:T(8,128)(2,1)}), bf16[7168,128]{1,0:T(8,128)(2,1)}) %all-gather.11.cloned.1.call-update) | async-done | bytes 1835024 | tf_op jit(solution)/shard_map/all_gather | solution.py:56
  57.3 7.7 %fusion.16 = f32[512,896]{1,0:T(8,128)} fusion(bf16[128,896]{1,0:T(8,128)(2,1)S(1)} %copy-done.21, bf16[7168,128]{1,0:T(8,128)(2,1)} %all-gather.11.cloned.1.call-done, bf16[512,7168]{1,0:T(8,128)(2,1)} %param.15, f32[7168]{0:T(1024)S(1)} %copy-done.23, f32[512]{0:T(512)S(1)} %add_rsqrt_fusion), kind=kOutput, calls=%fused_computation.31 | convolution fusion | flops 1071710208 | bytes 11270144 | tf_op jit(solution)/shard_map/dot_general | solution.py:65
  65.0 37.2 %all-gather.7.cloned.1.call-done = bf16[7168,128]{1,0:T(8,128)(2,1)} async-done(((bf16[224,128]{1,0:T(8,128)(2,1)}), bf16[7168,128]{1,0:T(8,128)(2,1)}) %all-gather.7.cloned.1.call-update) | async-done | bytes 1835024 | tf_op jit(solution)/shard_map/all_gather | solution.py:61
  102.1 7.6 %fusion.17 = f32[512,896]{1,0:T(8,128)} fusion(bf16[128,896]{1,0:T(8,128)(2,1)S(1)} %copy-done.22, bf16[7168,128]{1,0:T(8,128)(2,1)} %all-gather.7.cloned.1.call-done, bf16[512,7168]{1,0:T(8,128)(2,1)} %param.15, f32[7168]{0:T(1024)S(1)} %copy-done.23, f32[512]{0:T(512)S(1)} %add_rsqrt_fusion), kind=kOutput, calls=%fused_computation.33 | convolution fusion | flops 1071710208 | bytes 11270144 | tf_op jit(solution)/shard_map/dot_general | solution.py:69
  109.8 57.4 %all-gather.9.cloned.1.call-done = bf16[7168,896]{1,0:T(8,128)(2,1)} async-done(((bf16[224,896]{1,0:T(8,128)(2,1)}), bf16[7168,896]{1,0:T(8,128)(2,1)}) %all-gather.9.cloned.1.call-update) | async-done | bytes 12845072 | tf_op jit(solution)/shard_map/all_gather | solution.py:55
  167.2 14.2 %add_convert_fusion = bf16[512,896]{1,0:T(8,128)(2,1)S(1)} fusion(f32[512,896]{1,0:T(8,128)} %fusion.16, bf16[7168,896]{1,0:T(8,128)(2,1)} %all-gather.9.cloned.1.call-done, bf16[512,7168]{1,0:T(8,128)(2,1)} %param.15, f32[7168]{0:T(1024)S(1)} %copy-done.23, f32[512]{0:T(512)S(1)} %add_rsqrt_fusion), kind=kOutput, calls=%fused_computation.27 | convolution fusion | flops 6592266240 | bytes 22968320 | tf_op jit(solution)/shard_map/dot_general | solution.py:50
  181.4 51.0 %all-gather.5.cloned.1.call-done = bf16[7168,896]{1,0:T(8,128)(2,1)} async-done(((bf16[224,896]{1,0:T(8,128)(2,1)}), bf16[7168,896]{1,0:T(8,128)(2,1)}) %all-gather.5.cloned.1.call-update) | async-done | bytes 12845072 | tf_op jit(solution)/shard_map/all_gather | solution.py:60
  232.4 14.2 %add_convert_fusion.1 = bf16[512,896]{1,0:T(8,128)(2,1)S(1)} fusion(f32[512,896]{1,0:T(8,128)} %fusion.17, bf16[7168,896]{1,0:T(8,128)(2,1)} %all-gather.5.cloned.1.call-done, bf16[512,7168]{1,0:T(8,128)(2,1)} %param.15, f32[7168]{0:T(1024)S(1)} %copy-done.23, f32[512]{0:T(512)S(1)} %add_rsqrt_fusion), kind=kOutput, calls=%fused_computation.28 | convolution fusion | flops 6592266240 | bytes 22968320 | tf_op jit(solution)/shard_map/dot_general | solution.py:50
  248.9 2.8 collective-permute-start
  254.1 4.4 collective-permute-start.1
  260.7 3.7 collective-permute-start.2
  280.2 9.8 %scatter_fusion = bf16[64,8,2,896]{3,1,2,0:T(8,128)(2,1)} fusion(bf16[64,8,2,896]{3,1,2,0:T(8,128)(2,1)} %broadcast_in_dim.68, s32[64]{0:T(128)S(1)} %compare_select_fusion, bf16[64,8,2,896]{3,1,2,0:T(8,128)(2,1)} %pad_maximum_fusion.1), kind=kCustom, calls=%fused_computation | custom fusion | bytes 5505280 | tf_op jit(solution)/shard_map/scatter | solution.py:119
  290.0 5.0 all-to-all-start
  296.1 4.5 fusion.5
  305.4 35.5 %collective-permute-done.1 = bf16[512,2,896]{2,0,1:T(8,128)(2,1)} collective-permute-done((bf16[512,2,896]{2,0,1:T(8,128)(2,1)}, bf16[512,2,896]{2,0,1:T(8,128)(2,1)}, u32[]{:S(2)}, u32[]{:S(2)}) %collective-permute-start.1) | collective-permute-done | bytes 1835040 | tf_op jit(solution)/shard_map/ppermute | solution.py:15
  340.9 2.8 fusion.42
  346.0 34.3 %collective-permute-done.2 = bf16[512,2,896]{2,0,1:T(8,128)(2,1)} collective-permute-done((bf16[512,2,896]{2,0,1:T(8,128)(2,1)}, bf16[512,2,896]{2,0,1:T(8,128)(2,1)}, u32[]{:S(2)}, u32[]{:S(2)}) %collective-permute-start.2) | collective-permute-done | bytes 1835040 | tf_op jit(solution)/shard_map/ppermute | solution.py:15
  380.3 2.9 fusion.41
  385.4 22.1 %collective-permute-done.3 = bf16[512,2,896]{2,0,1:T(8,128)(2,1)} collective-permute-done((bf16[512,2,896]{2,0,1:T(8,128)(2,1)}, bf16[512,2,896]{2,0,1:T(8,128)(2,1)}, u32[]{:S(2)}, u32[]{:S(2)}) %collective-permute-start.3) | collective-permute-done | bytes 1835040 | tf_op jit(solution)/shard_map/ppermute | solution.py:15
  407.5 2.9 fusion.40
  419.8 4.6 fusion.7
  424.4 3.0 fusion.9
  427.4 3.0 fusion.11
  430.5 2.9 fusion.13
  433.5 8.9 %fusion = f32[4,512]{1,0:T(4,128)S(1)} fusion(f32[4,512,2560]{1,2,0:T(8,128)} %get-tuple-element.30, f32[4,512]{1,0:T(4,128)S(1)} %maximum_maximum_fusion), kind=kLoop, calls=%fused_computation.3 | loop fusion | flops 10483712 | bytes 20987904 | tf_op jit(solution)/shard_map/reduce_sum | solution.py:107
  443.6 9.2 %fusion.15 = bf16[4,224,512]{2,1,0:T(8,128)(2,1)S(1)} fusion(bf16[2560,4,224]{0,2,1:T(8,128)(2,1)S(1)} %constant_dynamic-update-slice_fusion, f32[4,512,2560]{1,2,0:T(8,128)} %get-tuple-element.30, f32[4,512]{1,0:T(4,128)S(1)} %fusion, f32[4,512]{1,0:T(4,128)S(1)} %maximum_maximum_fusion), kind=kOutput, calls=%fused_computation.29 | convolution fusion | flops 2364997632 | bytes 26492928 | tf_op jit(solution)/shard_map/hqk,khd->qhd/dot_general | solution.py:108
  452.8 4.8 fusion.18
  457.6 25.9 %all-to-all-done = bf16[64,8,2,896]{3,1,2,0:T(8,128)(2,1)} async-done(((bf16[64,8,2,896]{3,1,2,0:T(8,128)(2,1)}), bf16[64,8,2,896]{3,1,2,0:T(8,128)(2,1)}, u32[]{:S(2)}, u32[]{:S(2)}) %all-to-all-start) | async-done | bytes 1835040 | tf_op jit(solution)/shard_map/all_to_all | solution.py:120
  483.5 4.2 copy.70
  487.7 178.0 %all-reduce.2.cloned.1.call-done = f32[16,3584]{1,0:T(8,128)} async-done(((f32[16,3584]{1,0:T(8,128)}), f32[16,3584]{1,0:T(8,128)}) %all-reduce.2.cloned.1.call-update) | async-done | bytes 229392 | tf_op jit(solution)/shard_map/psum | solution.py:133
  670.2 63.3 %pmax.7 = f32[16]{0:T(128)} all-reduce(f32[16]{0:T(128)S(1)} %convolution_reduce_fusion), channel_id=1, replica_groups=mesh['seq'=32,'tp'=4] {'seq','tp'}, use_global_device_ids=true, to_apply=%region_20.21 | all-reduce | flops 16 | bytes 128 | tf_op jit(solution)/shard_map/pmax | solution.py:141
  (108 shorter events, 54.2 us)
Async XLA Ops:
  7.2 660.1 %copy-start = (bf16[250,3584]{1,0:T(8,128)(2,1)S(1)}, bf16[250,3584]{1,0:T(8,128)(2,1)}, u32[]{:S(2)}) copy-start(bf16[250,3584]{1,0:T(8,128)(2,1)} %param.26) | copy-start | bytes 5376004
  7.2 50.1 %copy-start.23 = (f32[7168]{0:T(1024)S(1)}, f32[7168]{0:T(1024)}, u32[]{:S(2)}) copy-start(f32[7168]{0:T(1024)} %param.16) | copy-start | bytes 86020
  7.2 50.1 %copy-start.21 = (bf16[128,896]{1,0:T(8,128)(2,1)S(1)}, bf16[128,896]{1,0:T(8,128)(2,1)}, u32[]{:S(2)}) copy-start(bf16[128,896]{1,0:T(8,128)(2,1)} %param.21) | copy-start | bytes 688132
  7.2 50.1 %all-gather.11.cloned.1.call-start = ((), (), s32[]{:S(2)}) async-start(), calls=%async_computation.4 | async-start | bytes 1892352 | tf_op jit(solution)/shard_map/all_gather | solution.py:56
  7.9 94.2 %all-gather.7.cloned.1.call-start = ((), (), s32[]{:S(2)}) async-start(), calls=%async_computation.2 | async-start | bytes 1892352 | tf_op jit(solution)/shard_map/all_gather | solution.py:61
  8.7 158.5 %all-gather.9.cloned.1.call-start = ((), (), s32[]{:S(2)}) async-start(), calls=%async_computation.3 | async-start | bytes 13246464 | tf_op jit(solution)/shard_map/all_gather | solution.py:55
  9.4 222.9 %all-gather.5.cloned.1.call-start = ((), (), s32[]{:S(2)}) async-start(), calls=%async_computation.1 | async-start | bytes 13246464 | tf_op jit(solution)/shard_map/all_gather | solution.py:60
  10.8 54.1 %copy-start.20 = (s32[12,1]{0,1:T(1,128)}, s32[12,1]{0,1:T(1,128)S(1)}, u32[]{:S(2)}) copy-start(s32[12,1]{0,1:T(1,128)S(1)} %reduce-window.7) | copy-start | bytes 148
  18.0 84.1 %copy-start.22 = (bf16[128,896]{1,0:T(8,128)(2,1)S(1)}, bf16[128,896]{1,0:T(8,128)(2,1)}, u32[]{:S(2)}) copy-start(bf16[128,896]{1,0:T(8,128)(2,1)} %param.22) | copy-start | bytes 688132
  232.3 19.4 %copy-start.11 = (s32[512]{0:T(512)S(1)}, s32[512]{0:T(512)}, u32[]{:S(2)}) copy-start(s32[512]{0:T(512)} %copy-done.10) | copy-start | bytes 6148
  232.4 19.4 %copy-start.13 = (s32[512]{0:T(512)S(1)}, s32[512]{0:T(512)}, u32[]{:S(2)}) copy-start(s32[512]{0:T(512)} %copy-done.12) | copy-start | bytes 6148
  232.4 19.5 %copy-start.15 = (s32[512]{0:T(512)S(1)}, s32[512]{0:T(512)}, u32[]{:S(2)}) copy-start(s32[512]{0:T(512)} %compare_select_fusion.1) | copy-start | bytes 6148
  232.4 19.5 %copy-start.16 = (s32[512]{0:T(512)S(1)}, s32[512]{0:T(512)}, u32[]{:S(2)}) copy-start(s32[512]{0:T(512)} %compare_select_fusion.2) | copy-start | bytes 6148
  232.4 19.5 %copy-start.17 = (s32[512]{0:T(512)S(1)}, s32[512]{0:T(512)}, u32[]{:S(2)}) copy-start(s32[512]{0:T(512)} %compare_select_fusion.3) | copy-start | bytes 6148
  232.4 19.5 %copy-start.18 = (s32[512]{0:T(512)S(1)}, s32[512]{0:T(512)}, u32[]{:S(2)}) copy-start(s32[512]{0:T(512)} %compare_select_fusion.4) | copy-start | bytes 6148
  246.6 12.0 %copy-start.19 = (s32[64]{0:T(128)S(1)}, s32[64]{0:T(128)}, u32[]{:S(2)}) copy-start(s32[64]{0:T(128)} %param.29) | copy-start | bytes 772
  248.9 51.7 %collective-permute-start = (bf16[512,2,896]{2,0,1:T(8,128)(2,1)}, bf16[512,2,896]{2,0,1:T(8,128)(2,1)}, u32[]{:S(2)}, u32[]{:S(2)}) collective-permute-start(bf16[512,2,896]{2,0,1:T(8,128)(2,1)} %pad_maximum_fusion), channel_id=1, source_target_pairs={{0,4},{4,8},{8,12},{12,16},{16,20},{20,24},{24,28},{28,32},{32,36}... | collective-permute-start | bytes 5505032 | tf_op jit(solution)/shard_map/ppermute | solution.py:15
  254.1 86.8 %collective-permute-start.1 = (bf16[512,2,896]{2,0,1:T(8,128)(2,1)}, bf16[512,2,896]{2,0,1:T(8,128)(2,1)}, u32[]{:S(2)}, u32[]{:S(2)}) collective-permute-start(bf16[512,2,896]{2,0,1:T(8,128)(2,1)} %pad_maximum_fusion), channel_id=1, source_target_pairs={{0,8},{4,12},{8,16},{12,20},{16,24},{20,28},{24,32},{28,36},{32,40... | collective-permute-start | bytes 5505032 | tf_op jit(solution)/shard_map/ppermute | solution.py:15
  260.7 119.6 %collective-permute-start.2 = (bf16[512,2,896]{2,0,1:T(8,128)(2,1)}, bf16[512,2,896]{2,0,1:T(8,128)(2,1)}, u32[]{:S(2)}, u32[]{:S(2)}) collective-permute-start(bf16[512,2,896]{2,0,1:T(8,128)(2,1)} %pad_maximum_fusion), channel_id=1, source_target_pairs={{0,12},{4,16},{8,20},{12,24},{16,28},{20,32},{24,36},{28,40},{32,4... | collective-permute-start | bytes 5505032 | tf_op jit(solution)/shard_map/ppermute | solution.py:15
  266.0 141.5 %collective-permute-start.3 = (bf16[512,2,896]{2,0,1:T(8,128)(2,1)}, bf16[512,2,896]{2,0,1:T(8,128)(2,1)}, u32[]{:S(2)}, u32[]{:S(2)}) collective-permute-start(bf16[512,2,896]{2,0,1:T(8,128)(2,1)} %pad_maximum_fusion), channel_id=1, source_target_pairs={{0,16},{4,20},{8,24},{12,28},{16,32},{20,36},{24,40},{28,44},{32,4... | collective-permute-start | bytes 5505032 | tf_op jit(solution)/shard_map/ppermute | solution.py:15
  280.2 14.9 %copy-start.5 = (bf16[512,896]{0,1:T(8,128)(2,1)S(1)}, bf16[512,896]{0,1:T(8,128)(2,1)}, u32[]{:S(2)}) copy-start(bf16[512,896]{0,1:T(8,128)(2,1)} %copy.55) | copy-start | bytes 2752516
  290.0 193.5 %all-to-all-start = ((bf16[64,8,2,896]{3,1,2,0:T(8,128)(2,1)}), bf16[64,8,2,896]{3,1,2,0:T(8,128)(2,1)}, u32[]{:S(2)}, u32[]{:S(2)}) async-start(bf16[64,8,2,896]{3,1,2,0:T(8,128)(2,1)} %scatter_fusion), calls=%async_computation | async-start | bytes 3670016 | tf_op jit(solution)/shard_map/all_to_all | solution.py:120
  295.0 370.6 %all-reduce.2.cloned.1.call-start = ((), (), s32[]{:S(2)}) async-start(), calls=%async_computation.5 | async-start | bytes 458752 | tf_op jit(solution)/shard_map/psum | solution.py:133
  419.8 4.6 copy-start.6
  419.8 4.6 copy-start.7
  424.4 3.0 copy-start.8
  427.4 3.0 copy-start.9
  430.5 11.9 %slice-start = ((s8[4587520]{0:T(1024)(128)(4,1)}), s8[4194304]{0:T(1024)(128)(4,1)S(1)}, s32[]{:S(2)}) async-start(s8[4587520]{0:T(1024)(128)(4,1)} %bitcast.96), calls=%async_computation.6 | async-start | bytes 8388608
  433.4 8.9 %copy-start.2 = (bf16[512,1,896]{0,2,1:T(8,128)(2,1)S(1)}, bf16[512,1,896]{0,2,1:T(8,128)(2,1)}, u32[]{:S(2)}) copy-start(bf16[512,1,896]{0,2,1:T(8,128)(2,1)} %copy.56) | copy-start | bytes 2752516
  433.4 8.9 %slice-start.1 = ((s8[4587520]{0:T(1024)(128)(4,1)}), s8[393216]{0:T(1024)(128)(4,1)S(1)}, s32[]{:S(2)}) async-start(s8[4587520]{0:T(1024)(128)(4,1)} %bitcast.96), calls=%async_computation.7 | async-start | bytes 786432
  433.4 9.1 %copy-start.3 = (bf16[512,1,896]{0,2,1:T(8,128)(2,1)S(1)}, bf16[512,1,896]{0,2,1:T(8,128)(2,1)}, u32[]{:S(2)}) copy-start(bf16[512,1,896]{0,2,1:T(8,128)(2,1)} %copy.58) | copy-start | bytes 2752516
  452.8 214.5 %copy-start.14 = (f32[3584]{0:T(1024)S(1)}, f32[3584]{0:T(1024)}, u32[]{:S(2)}) copy-start(f32[3584]{0:T(1024)} %param.25) | copy-start | bytes 43012
  (4 other events, 7.1 us)
Sparse Core Ops, SparseCore 0:
  10.3 46.9 all-gather.10
  59.5 42.5 all-gather.6
  104.4 62.7 all-gather.8
  169.3 63.0 all-gather.4
  457.7 207.8 all-reduce.1
where the time goes:
time: 741 us; the launch traced here: 740 us
  waiting for transfers between devices  483 us (65%)
  matrix products  77.4 us (10%)
  blocking collectives  63.3 us (9%)
  local copies, waits for them, and re-layouts  53 us (7%)
  other arithmetic  30 us (4%)
  starting transfers between devices  19 us (3%)
  between operations  14.1 us (2%)
    psum x1, waiting for transfers between devices, local(): state = lax.psum(partial_state, ('seq', 'tp'))  178 us
    ppermute x4, waiting for transfers between devices, passed_along(): lax.ppermute(value, axis, [(source, source + steps) for source in range(l...  91.9 us
    pmax x1, blocking collectives, local(): logit_max = lax.pmax(jnp.max(logits, axis=1), ('seq', 'tp'))  63.3 us
    all_gather x1, waiting for transfers between devices, local(): lax.all_gather(k_weight, 'seq', axis=0, tiled=True)  57.4 us
    all_gather x1, waiting for transfers between devices, local(): lax.all_gather(v_weight, 'seq', axis=0, tiled=True)  51 us
    all_gather x1, waiting for transfers between devices, local(): lax.all_gather(k_down, 'seq', axis=0, tiled=True)  39.3 us
    all_gather x1, waiting for transfers between devices, local(): lax.all_gather(v_down, 'seq', axis=0, tiled=True)  37.2 us
    dot_general x2, matrix products, add_pair(): jnp.dot(normed, w_piece, preferred_element_type=jnp.float32)  28.4 us
  transfers between devices with their start and end apart: 10, of which 9 were waited for; matrix products, arithmetic and copies ran while one was open for 19% of the time, Pallas kernels for 0%

commit v1 on v0

--- a/solution.py
+++ b/solution.py
@@ -1,12 +1,17 @@
+import functools
+
 import jax
 import jax.numpy as jnp
 from jax import lax
+from jax.experimental import pallas as pl
+from jax.experimental.pallas import tpu as pltpu
 from jax.sharding import PartitionSpec as P
 
 HEAD = 224
 PAGE = 8
 LOOKBACK = 4
 NPROMPT = 12
+RING = 4
 
 
 def passed_along(value, axis, steps):
@@ -18,6 +23,422 @@
 def segment_of(positions, bounds):
     counted = jnp.sum((bounds[None, :] <= positions[:, None]).astype(jnp.int32), axis=1)
     return jnp.where(positions < 0, -1, counted)
+
+
+MESH = pl.DeviceIdType.MESH
+
+
+def place(zs):
+    s = lax.axis_index("seq")
+    core = s % 2
+    chip = s // 2
+    return core, chip % zs, chip // zs
+
+
+def seq_id(core, z, y, zs):
+    return (y * zs + z) * 2 + core
+
+
+def enter(peers):
+    barrier = pltpu.get_barrier_semaphore()
+    for peer in peers:
+        pl.semaphore_signal(barrier, inc=1, device_id=peer, device_id_type=MESH)
+    pl.semaphore_wait(barrier, len(peers))
+
+
+def tail_kernel(
+    zs,
+    ys,
+    tps,
+    picked_ref,
+    o_ref,
+    gain_ref,
+    un_ref,
+    norm_ref,
+    max_ref,
+    o_buf,
+    un_buf,
+    row_c,
+    row_z,
+    row_y,
+    sum_c,
+    sum_z,
+    parts,
+    states,
+    final_buf,
+    max_own,
+    max_got,
+    send,
+    recv,
+    local_sem,
+):
+    core, z, y = place(zs)
+    x = lax.axis_index("tp")
+    rows, width = picked_ref.shape
+    chunk = o_buf.shape[1]
+    load_o = pltpu.make_async_copy(
+        o_ref.at[:, pl.ds(pl.multiple_of(z * chunk, chunk), chunk)], o_buf, local_sem.at[0]
+    )
+    load_o.start()
+    load_u = pltpu.make_async_copy(un_ref, un_buf, local_sem.at[1])
+    load_u.start()
+    on_core = [{"seq": seq_id(1 - core, z, y, zs)}]
+    on_z = [{"seq": seq_id(core, (z + k) % zs, y, zs)} for k in range(1, zs)]
+    on_y = [{"seq": seq_id(core, z, (y + k) % ys, zs)} for k in range(1, ys)]
+    on_x = [{"tp": (x + k) % tps} for k in range(1, tps)]
+    enter(on_core + on_z + on_y + on_x)
+    used = [0]
+
+    def exchange(peers, source, target):
+        copies = []
+        for k, peer in enumerate(peers):
+            n = used[0]
+            used[0] = n + 1
+            copy = pltpu.make_async_remote_copy(
+                src_ref=source,
+                dst_ref=target(k),
+                send_sem=send.at[n],
+                recv_sem=recv.at[n],
+                device_id=peer,
+                device_id_type=MESH,
+            )
+            copy.start()
+            copies.append(copy)
+        return copies
+
+    def finish(copies):
+        for copy in copies:
+            copy.wait()
+
+    going = exchange(on_core, picked_ref, lambda k: row_c.at[k])
+    final_buf[...] = jnp.zeros_like(final_buf)
+    finish(going)
+    sum_c[...] = picked_ref[...] + row_c[0]
+    finish(exchange(on_z, sum_c, lambda k: row_z.at[k]))
+    total = sum_c[...]
+    for k in range(zs - 1):
+        total = total + row_z[k]
+    sum_z[...] = total
+    finish(exchange(on_y, sum_z, lambda k: row_y.at[k]))
+    for k in range(ys - 1):
+        total = total + row_y[k]
+    load_o.wait()
+    parts[x] = jnp.dot(total, o_buf[...], preferred_element_type=jnp.float32)
+    finish(exchange(on_x, parts.at[x], lambda k: parts.at[x]))
+    state = parts[0]
+    for k in range(1, tps):
+        state = state + parts[k]
+    states[z] = state
+    finish(exchange(on_z, states.at[z], lambda k: states.at[z]))
+    squares = jnp.zeros((rows, 1), jnp.float32)
+    for k in range(zs):
+        squares = squares + jnp.sum(states[k] * states[k], axis=1, keepdims=True)
+    norm_ref[...] = jnp.broadcast_to(jnp.sqrt(squares), norm_ref.shape)
+    inverse = lax.rsqrt(squares / (zs * chunk) + 1e-05)
+    for k in range(zs):
+        final_buf[k, 0:rows, :] = (
+            states[k] * inverse * gain_ref[:, k * chunk : (k + 1) * chunk]
+        ).astype(jnp.bfloat16)
+    load_u.wait()
+    logits = jnp.zeros((un_buf.shape[0], final_buf.shape[1]), jnp.float32)
+    for k in range(zs):
+        logits = logits + lax.dot_general(
+            un_buf[:, k * chunk : (k + 1) * chunk],
+            final_buf[k],
+            (((1,), (1,)), ((), ())),
+            preferred_element_type=jnp.float32,
+        )
+    best = jnp.broadcast_to(jnp.max(logits, axis=0, keepdims=True), max_ref.shape)
+    place_at = 0
+    for step, peers in enumerate((on_core, on_z, on_y, on_x)):
+        max_own[step] = best
+        start = place_at
+        finish(exchange(peers, max_own.at[step], lambda k: max_got.at[start + k]))
+        for k in range(len(peers)):
+            best = jnp.maximum(best, max_got[start + k])
+        place_at = place_at + len(peers)
+    max_ref[...] = best
+
+
+def tail(picked, o_weight, final_gain, unembed, zs, ys, tps):
+    rows, width = picked.shape
+    model = o_weight.shape[1]
+    chunk = model // zs
+    pads = 128
+    copies = (1 + zs + ys + tps - 3) * 2 + zs - 1
+    vmem = pl.BlockSpec(memory_space=pltpu.VMEM)
+    anywhere = pl.BlockSpec(memory_space=pl.ANY)
+    norm, best = pl.pallas_call(
+        functools.partial(tail_kernel, zs, ys, tps),
+        out_shape=(
+            jax.ShapeDtypeStruct((rows, 128), jnp.float32),
+            jax.ShapeDtypeStruct((8, pads), jnp.float32),
+        ),
+        in_specs=[vmem, anywhere, vmem, anywhere],
+        out_specs=(vmem, vmem),
+        scratch_shapes=[
+            pltpu.VMEM((width, chunk), jnp.bfloat16),
+            pltpu.VMEM(unembed.shape, jnp.bfloat16),
+            pltpu.VMEM((1, rows, width), jnp.bfloat16),
+            pltpu.VMEM((max(1, zs - 1), rows, width), jnp.bfloat16),
+            pltpu.VMEM((max(1, ys - 1), rows, width), jnp.bfloat16),
+            pltpu.VMEM((rows, width), jnp.bfloat16),
+            pltpu.VMEM((rows, width), jnp.bfloat16),
+            pltpu.VMEM((tps, rows, chunk), jnp.float32),
+            pltpu.VMEM((zs, rows, chunk), jnp.float32),
+            pltpu.VMEM((zs, pads, chunk), jnp.bfloat16),
+            pltpu.VMEM((4, 8, pads), jnp.float32),
+            pltpu.VMEM((1 + zs + ys + tps - 3, 8, pads), jnp.float32),
+            pltpu.SemaphoreType.DMA((copies,)),
+            pltpu.SemaphoreType.DMA((copies,)),
+            pltpu.SemaphoreType.DMA((2,)),
+        ],
+        compiler_params=pltpu.CompilerParams(collective_id=0, has_side_effects=True),
+        name="tail",
+    )(picked, o_weight, final_gain.reshape(1, model), unembed)
+    return norm[:, 0], best[0, :rows]
+
+
+ORDER = (
+    (0, 0),
+    (1, 0),
+    (3, 0),
+    (0, 1),
+    (0, 3),
+    (2, 0),
+    (1, 1),
+    (1, 3),
+    (3, 1),
+    (3, 3),
+    (0, 2),
+    (2, 1),
+    (2, 3),
+    (1, 2),
+    (3, 2),
+    (2, 2),
+)
+
+
+def project_kernel(
+    ring,
+    hidden_ref,
+    gain_ref,
+    kw_ref,
+    vw_ref,
+    kd_ref,
+    vd_ref,
+    ku_ref,
+    vu_ref,
+    kv_ref,
+    held,
+    normed,
+    total,
+    send,
+    recv,
+    sib_send,
+    sib_recv,
+    local_sem,
+):
+    core, z, y = place(ring)
+    rows = hidden_ref.shape[0]
+    depth, width = kw_ref.shape
+    rank = kd_ref.shape[1]
+    half = depth // 2
+    steps = len(ORDER)
+    slot_of = {pair: n for n, pair in enumerate(ORDER)}
+
+    def device(first, second):
+        to_z = (z + first * (1 - core) + second * core + ring) % ring
+        to_y = (y + first * core + second * (1 - core) + ring) % ring
+        return {"seq": seq_id(core, to_z, to_y, ring)}
+
+    sibling = {"seq": seq_id(1 - core, z, y, ring)}
+    loads = []
+    at = 0
+    for n, ref in enumerate((kw_ref, vw_ref, kd_ref, vd_ref)):
+        wide = ref.shape[1]
+        load = pltpu.make_async_copy(ref, held.at[0, 0, :, at : at + wide], local_sem.at[n])
+        load.start()
+        loads.append(load)
+        at = at + wide
+    enter([device(1, 0), device(-1, 0), device(0, 1), device(0, -1), sibling])
+    for load in loads:
+        load.wait()
+
+    plan = {}
+    count = 0
+    for slot, (i, j) in enumerate(ORDER):
+        sends = []
+        if (i, j) == (0, 0):
+            sends += [((1, 0), (3, 0), 0), ((-1, 0), (1, 0), 0)]
+        if j == 0:
+            sends += [((0, 1), (i, 3), 0), ((0, -1), (i, 1), 0)]
+        if (i, j) == (0, 0):
+            sends += [((1, 0), (3, 0), 1), ((-1, 0), (1, 0), 1)]
+        if (i, j) == (3, 0):
+            sends += [((1, 0), (2, 0), 0)]
+        if (i, j) == (1, 0):
+            sends += [((-1, 0), (2, 0), 1)]
+        if j == 0:
+            sends += [((0, 1), (i, 3), 1), ((0, -1), (i, 1), 1)]
+        if j == 3:
+            sends += [((0, 1), (i, 2), 0)]
+        if j == 1:
+            sends += [((0, -1), (i, 2), 1)]
+        plan[slot] = []
+        for step, target, part in sends:
+            plan[slot].append((step, slot_of[target], part, count))
+            count = count + 1
+
+    def piece(net, slot, part):
+        return held.at[net, slot, pl.ds(part * half, half), :]
+
+    def copy_out(slot, entry):
+        step, target, part, n = entry
+        return pltpu.make_async_remote_copy(
+            src_ref=piece(0, slot, part),
+            dst_ref=piece(0, target, part),
+            send_sem=send.at[n],
+            recv_sem=recv.at[target, part],
+            device_id=device(*step),
+            device_id_type=MESH,
+        )
+
+    def beside(slot):
+        return pltpu.make_async_remote_copy(
+            src_ref=held.at[0, slot],
+            dst_ref=held.at[1, slot],
+            send_sem=sib_send.at[slot],
+            recv_sem=sib_recv.at[slot],
+            device_id=sibling,
+            device_id_type=MESH,
+        )
+
+    for entry in plan[0]:
+        copy_out(0, entry).start()
+
+    block = min(rows, 64)
+    group = 4 * depth
+    groups = hidden_ref.shape[1] // group
+
+    @pl.loop(0, rows // block)
+    def _(b):
+        at_rows = pl.ds(pl.multiple_of(b * block, block), block)
+        squares = jnp.zeros((block, 1), jnp.float32)
+        for g in range(groups):
+            wide = hidden_ref[at_rows, g * group : (g + 1) * group].astype(jnp.float32)
+            squares = squares + jnp.sum(wide * wide, axis=1, keepdims=True)
+        inverse = lax.rsqrt(squares / (groups * group) + 1e-05)
+        for g in range(groups):
+            wide = hidden_ref[at_rows, g * group : (g + 1) * group].astype(jnp.float32)
+            scaled = wide * inverse * gain_ref[:, g * group : (g + 1) * group]
+            for k in range(4):
+                normed[g * 4 + k, at_rows, :] = scaled[:, k * depth : (k + 1) * depth].astype(
+                    jnp.bfloat16
+                )
+
+    tile = min(512, total.shape[1])
+
+    def add(net, slot, source):
+        left = normed[source]
+        for t in range(total.shape[1] // tile):
+            cols = slice(t * tile, (t + 1) * tile)
+            total[:, cols] += jnp.dot(
+                left, held[net, slot, :, cols], preferred_element_type=jnp.float32
+            )
+
+    total[...] = jnp.zeros_like(total)
+
+    @pl.loop(0, steps)
+    def _(e):
+        @pl.when(e > 0)
+        def _():
+            for part in range(2):
+                pltpu.make_async_remote_copy(
+                    src_ref=piece(0, e, part),
+                    dst_ref=piece(0, e, part),
+                    send_sem=send.at[0],
+                    recv_sem=recv.at[e, part],
+                    device_id=sibling,
+                    device_id_type=MESH,
+                ).wait_recv()
+
+        for slot in range(1, steps):
+            if plan[slot]:
+
+                @pl.when(e == slot)
+                def _(slot=slot):
+                    for entry in plan[slot]:
+                        copy_out(slot, entry).start()
+
+        beside(e).start()
+        first, second = 0, 0
+        for slot, (i, j) in enumerate(ORDER):
+            first = first + jnp.where(e == slot, i, 0)
+            second = second + jnp.where(e == slot, j, 0)
+
+        def source(kind):
+            from_z = (z + first * (1 - kind) + second * kind) % ring
+            from_y = (y + first * kind + second * (1 - kind)) % ring
+            return seq_id(kind, from_z, from_y, ring)
+
+        add(0, e, source(core))
+        beside(e).wait_recv()
+        add(1, e, source(1 - core))
+
+    @pl.loop(0, rows // block)
+    def _(b):
+        at_rows = pl.ds(pl.multiple_of(b * block, block), block)
+        for n, up in enumerate((ku_ref, vu_ref)):
+            low = total[at_rows, 2 * width + n * rank : 2 * width + (n + 1) * rank]
+            kv_ref[at_rows, n * width : (n + 1) * width] = (
+                total[at_rows, n * width : (n + 1) * width]
+                + jnp.dot(low.astype(jnp.bfloat16), up[...], preferred_element_type=jnp.float32)
+            ).astype(jnp.bfloat16)
+
+    for slot in range(steps):
+        for entry in plan[slot]:
+            copy_out(slot, entry).wait_send()
+        beside(slot).wait_send()
+
+
+def project(hidden_cat, norm_gain, k_weight, v_weight, k_down, v_down, k_up, v_up, ring):
+    rows, wide = hidden_cat.shape
+    depth, width = k_weight.shape
+    rank = k_down.shape[1]
+    columns = 2 * (width + rank)
+    steps = ring * ring
+    vmem = pl.BlockSpec(memory_space=pltpu.VMEM)
+    anywhere = pl.BlockSpec(memory_space=pl.ANY)
+    return pl.pallas_call(
+        functools.partial(project_kernel, ring),
+        out_shape=jax.ShapeDtypeStruct((rows, 2 * width), jnp.bfloat16),
+        in_specs=[vmem, vmem, anywhere, anywhere, anywhere, anywhere, vmem, vmem],
+        out_specs=vmem,
+        scratch_shapes=[
+            pltpu.VMEM((2, steps, depth, columns), jnp.bfloat16),
+            pltpu.VMEM((2 * steps, rows, depth), jnp.bfloat16),
+            pltpu.VMEM((rows, columns), jnp.float32),
+            pltpu.SemaphoreType.DMA((32,)),
+            pltpu.SemaphoreType.DMA((steps, 2)),
+            pltpu.SemaphoreType.DMA((steps,)),
+            pltpu.SemaphoreType.DMA((steps,)),
+            pltpu.SemaphoreType.DMA((4,)),
+        ],
+        compiler_params=pltpu.CompilerParams(
+            collective_id=1, has_side_effects=True, vmem_limit_bytes=62 << 20
+        ),
+        name="project",
+    )(
+        hidden_cat,
+        norm_gain.reshape(1, wide),
+        k_weight,
+        v_weight,
+        k_down,
+        v_down,
+        k_up,
+        v_up,
+    )
 
 
 def local(
@@ -41,34 +462,10 @@
     width = k_weight.shape[1]
     heads_here = width // HEAD
     seq_count = lax.axis_size("seq")
-    wide = hidden_cat.astype(jnp.float32)
-    inverse = lax.rsqrt(jnp.mean(wide * wide, axis=1, keepdims=True) + 1e-05)
-    normed = (wide * inverse * norm_gain).astype(jnp.bfloat16)
-
-    def add_pair(w_piece, d_piece):
-        return (
-            jnp.dot(normed, w_piece, preferred_element_type=jnp.float32),
-            jnp.dot(normed, d_piece, preferred_element_type=jnp.float32),
-        )
-
-    pieces = (
-        lax.all_gather(k_weight, "seq", axis=0, tiled=True),
-        lax.all_gather(k_down, "seq", axis=0, tiled=True),
-    )
-    key_base, key_low = add_pair(pieces[0], pieces[1])
-    pieces = (
-        lax.all_gather(v_weight, "seq", axis=0, tiled=True),
-        lax.all_gather(v_down, "seq", axis=0, tiled=True),
-    )
-    value_base, value_low = add_pair(pieces[0], pieces[1])
-    key_rows = (
-        key_base + jnp.dot(key_low.astype(jnp.bfloat16), k_up, preferred_element_type=jnp.float32)
-    ).astype(jnp.bfloat16)
-    value_rows = (
-        value_base
-        + jnp.dot(value_low.astype(jnp.bfloat16), v_up, preferred_element_type=jnp.float32)
-    ).astype(jnp.bfloat16)
-    local_kv = jnp.stack([key_rows, value_rows], axis=1)
+    local_rows = project(
+        hidden_cat, norm_gain, k_weight, v_weight, k_down, v_down, k_up, v_up, RING
+    )
+    local_kv = local_rows.reshape(rows_here, 2, width)
     kv_blocks = [local_kv]
     for offset in range(1, LOOKBACK + 1):
         kv_blocks.append(passed_along(local_kv, "seq", offset))
@@ -129,16 +526,9 @@
     )
     selector = (request_pos[:, None] == query_pos[None, :]).astype(jnp.bfloat16)
     picked = jnp.dot(selector, attended, preferred_element_type=jnp.float32).astype(jnp.bfloat16)
-    partial_state = jnp.dot(picked, o_weight, preferred_element_type=jnp.float32)
-    state = lax.psum(partial_state, ("seq", "tp"))
-    state_norm = jnp.sqrt(jnp.sum(state * state, axis=1))
-    final = (
-        state * lax.rsqrt(jnp.mean(state * state, axis=1, keepdims=True) + 1e-05) * final_gain
-    ).astype(jnp.bfloat16)
-    logits = lax.dot_general(
-        final, unembed, (((1,), (1,)), ((), ())), preferred_element_type=jnp.float32
-    )
-    logit_max = lax.pmax(jnp.max(logits, axis=1), ("seq", "tp"))
+    state_norm, logit_max = tail(
+        picked, o_weight, final_gain, unembed, RING, RING, lax.axis_size("tp")
+    )
     return (attended, kv_cache, state_norm, logit_max)
 
 

time: 741 us -> 425 us (0.57)
  waiting for transfers between devices: 483 us -> 117 us
  Pallas kernels: 0 us -> 128 us
  blocking collectives: 63.3 us -> 0 us
  local copies, waits for them, and re-layouts: 53 us -> 115 us
  matrix products: 77.4 us -> 26.4 us
  other arithmetic: 30 us -> 15.4 us
  between operations: 14.1 us -> 0.9 us
    all_gather x4 -> x0, waiting for transfers between devices: 185 us -> none  [the longest x1 57.4 us: local(): lax.all_gather(k_weight, 'seq', axis=0, tiled=True)]
    psum x1 -> x0, waiting for transfers between devices: 178 us -> none  [local(): state = lax.psum(partial_state, ('seq', 'tp'))]
    pallas_call x0 -> x2, Pallas kernels: none -> 128 us  [the longest x1 93.8 us: project(): pl.pallas_call(functools.partial(project_kernel, ring), out_shape=jax.Sha...]
    ppermute x4, waiting for transfers between devices: 91.9 us -> 0.01 us  [passed_along(): lax.ppermute(value, axis, [(source, source + steps) for source in range(l...]
    all_to_all x1, waiting for transfers between devices: 25.9 us -> 117 us  [local(): lax.all_to_all(outgoing, 'seq', split_axis=0, concat_axis=0, tiled=True)]
    pmax x1 -> x0, blocking collectives: 63.3 us -> none  [local(): logit_max = lax.pmax(jnp.max(logits, axis=1), ('seq', 'tp'))]
    dot_general x6 -> x1, matrix products: 50.2 us -> 0.99 us  [local(): jnp.dot(selector, attended, preferred_element_type=jnp.float32)]
    slice x8 -> x10, local copies, waits for them, and re-layouts: 20 us -> 58.6 us  [local(): key_block = kv_blocks[offset][:, 0].reshape(rows_here, heads_here, HEAD)]
  transfers between devices with their start and end apart: 10 -> 5, of which waited for: 9 -> 1; matrix products, arithmetic and copies ran while one was open for 19% -> 23% of each run, Pallas kernels for 0% -> 0%
where the time goes in v1:
time: 425 us; the launch traced here: 422 us
  Pallas kernels  128 us (30%)
  waiting for transfers between devices  117 us (28%)
  local copies, waits for them, and re-layouts  115 us (27%)
  matrix products  26.4 us (6%)
  starting transfers between devices  19.9 us (5%)
  other arithmetic  15.4 us (4%)
    all_to_all x1, waiting for transfers between devices, local(): lax.all_to_all(outgoing, 'seq', split_axis=0, concat_axis=0, tiled=True)  117 us
    pallas_call x1, Pallas kernels, project(): pl.pallas_call(functools.partial(project_kernel, ring), out_shape=jax.Sha...  93.8 us
    slice x10, local copies, waits for them, and re-layouts, local(): key_block = kv_blocks[offset][:, 0].reshape(rows_here, heads_here, HEAD)  58.6 us
    pallas_call x1, Pallas kernels, tail(): pl.pallas_call(functools.partial(tail_kernel, zs, ys, tps), out_shape=(ja...  34 us
    slice x5, local copies, waits for them, and re-layouts, local(): kv_blocks[offset][:, 1].reshape(rows_here, heads_here, HEAD)  23.3 us
    dot_general x5, matrix products, compute_scores(): jnp.einsum('qhd,khd->hqk', query_heads, key_block, preferred_element_type...  16.2 us
    ppermute x4, starting transfers between devices, passed_along(): lax.ppermute(value, axis, [(source, source + steps) for source in range(l...  13.8 us
    unnamed x41, local copies, waits for them, and re-layouts  13.7 us
  transfers between devices with their start and end apart: 5, of which 1 were waited for; matrix products, arithmetic and copies ran while one was open for 23% of the time, Pallas kernels for 0%

profile of v1, /device:TPU:1, one launch (start us, length us, event | category | flops | bytes accessed | tf_op | source)
XLA Modules:
  0.0 422.2 jit_solution(10795530539633138625)
XLA Ops:
  0.6 93.8 %project.1 = bf16[512,1792]{1,0:T(8,128)(2,1)} custom-call(bf16[512,7168]{1,0:T(8,128)(2,1)} %hidden_ref.1, f32[1,7168]{1,0:T(1,128)} %bitcast.84, bf16[224,896]{1,0:T(8,128)(2,1)} %kw_ref.1, bf16[224,896]{1,0:T(8,128)(2,1)} %vw_ref.1, bf16[224,128]{1,0:T(8,128)(2,1)} %kd_ref.1, bf16[224,128]{1,0:T(8,128)(2,1)} %vd_ref.1, bf16[128,896]{1,0:T(8,128)(2,1)} %ku_ref.1, ...), custom_call_target="tpu_custom_call" | custom-call | tf_op jit(solution)/shard_map/project/pallas_call | solution.py:413
  94.5 3.8 reshape.407
  98.3 5.9 %collective-permute-start.3 = (bf16[512,2,896]{2,1,0:T(2,128)(2,1)S(1)}, bf16[512,2,896]{2,1,0:T(2,128)(2,1)}, u32[]{:S(2)}, u32[]{:S(2)}) collective-permute-start(bf16[512,2,896]{2,1,0:T(2,128)(2,1)S(1)} %reshape.407), channel_id=1, source_target_pairs={{0,16},{4,20},{8,24},{12,28},{16,32},{20,36},{24,40},{28,44},{32,4... | collective-permute-start | bytes 5505032 | tf_op jit(solution)/shard_map/ppermute | solution.py:20
  106.8 3.4 collective-permute-start.1
  113.9 9.8 %scatter_fusion = bf16[64,8,2,896]{3,1,2,0:T(8,128)(2,1)} fusion(bf16[64,8,2,896]{3,1,2,0:T(8,128)(2,1)} %broadcast_in_dim.116, s32[64]{0:T(128)S(1)} %compare_select_fusion, bf16[64,8,2,896]{3,1,2,0:T(8,128)(2,1)} %bitcast.64), kind=kCustom, calls=%fused_computation | custom fusion | bytes 5505280 | tf_op jit(solution)/shard_map/scatter | solution.py:516
  123.7 6.1 %all-to-all-start = ((bf16[64,8,2,896]{3,1,2,0:T(8,128)(2,1)}), bf16[64,8,2,896]{3,1,2,0:T(8,128)(2,1)}, u32[]{:S(2)}, u32[]{:S(2)}) async-start(bf16[64,8,2,896]{3,1,2,0:T(8,128)(2,1)} %scatter_fusion), calls=%async_computation | async-start | bytes 3670016 | tf_op jit(solution)/shard_map/all_to_all | solution.py:517
  129.9 4.4 %fusion.27 = (bf16[512,1,896]{2,1,0:T(2,128)(2,1)}, bf16[512,1,896]{2,1,0:T(2,128)(2,1)}) fusion(bf16[512,2,896]{2,1,0:T(2,128)(2,1)S(1)} %reshape.407), kind=kLoop, calls=%fused_computation.65 | loop fusion | bytes 3670016 | tf_op jit(solution)/shard_map/slice | solution.py:481
  136.3 4.4 %copy.51 = bf16[512,1,896]{0,2,1:T(8,128)(2,1)S(1)} copy(bf16[512,1,896]{2,1,0:T(2,128)(2,1)} %get-tuple-element.44) | data formatting | bytes 1835008 | tf_op jit(solution)/shard_map/slice | solution.py:499
  144.4 5.4 %copy.56 = bf16[512,1,896]{0,2,1:T(8,128)(2,1)} copy(bf16[512,1,896]{2,1,0:T(2,128)(2,1)} %get-tuple-element.43) | data formatting | bytes 1835008 | tf_op jit(solution)/shard_map/slice | solution.py:481
  149.9 2.9 compare_and_fusion
  152.8 4.2 fusion.2
  157.8 116.8 %all-to-all-done = bf16[64,8,2,896]{3,1,2,0:T(8,128)(2,1)} async-done(((bf16[64,8,2,896]{3,1,2,0:T(8,128)(2,1)}), bf16[64,8,2,896]{3,1,2,0:T(8,128)(2,1)}, u32[]{:S(2)}, u32[]{:S(2)}) %all-to-all-start) | async-done | bytes 1835040 | tf_op jit(solution)/shard_map/all_to_all | solution.py:517
  274.6 4.2 copy.64
  278.8 7.1 %fusion.23 = (bf16[512,1,896]{2,1,0:T(2,128)(2,1)}, bf16[512,1,896]{2,1,0:T(2,128)(2,1)}) fusion(bf16[512,2,896]{2,1,0:T(2,128)(2,1)} %collective-permute-done.3), kind=kLoop, calls=%fused_computation.61 | loop fusion | bytes 3670016 | tf_op jit(solution)/shard_map/slice | solution.py:481
  285.9 5.2 %copy.61 = bf16[512,1,896]{0,2,1:T(8,128)(2,1)} copy(bf16[512,1,896]{2,1,0:T(2,128)(2,1)} %get-tuple-element.35) | data formatting | bytes 1835008 | tf_op jit(solution)/shard_map/slice | solution.py:481
  291.1 4.6 %copy.55 = bf16[512,1,896]{0,2,1:T(8,128)(2,1)S(1)} copy(bf16[512,1,896]{2,1,0:T(2,128)(2,1)} %get-tuple-element.36) | data formatting | bytes 1835008 | tf_op jit(solution)/shard_map/slice | solution.py:499
  295.7 7.2 %fusion.24 = (bf16[512,1,896]{2,1,0:T(2,128)(2,1)}, bf16[512,1,896]{2,1,0:T(2,128)(2,1)}) fusion(bf16[512,2,896]{2,1,0:T(2,128)(2,1)} %collective-permute-done.2), kind=kLoop, calls=%fused_computation.62 | loop fusion | bytes 3670016 | tf_op jit(solution)/shard_map/slice | solution.py:481
  302.9 5.2 %copy.60 = bf16[512,1,896]{0,2,1:T(8,128)(2,1)} copy(bf16[512,1,896]{2,1,0:T(2,128)(2,1)} %get-tuple-element.37) | data formatting | bytes 1835008 | tf_op jit(solution)/shard_map/slice | solution.py:481
  308.1 5.2 %copy.54 = bf16[512,1,896]{0,2,1:T(8,128)(2,1)} copy(bf16[512,1,896]{2,1,0:T(2,128)(2,1)} %get-tuple-element.38) | data formatting | bytes 1835008 | tf_op jit(solution)/shard_map/slice | solution.py:499
  313.3 7.1 %fusion.25 = (bf16[512,1,896]{2,1,0:T(2,128)(2,1)}, bf16[512,1,896]{2,1,0:T(2,128)(2,1)}) fusion(bf16[512,2,896]{2,1,0:T(2,128)(2,1)} %collective-permute-done.1), kind=kLoop, calls=%fused_computation.63 | loop fusion | bytes 3670016 | tf_op jit(solution)/shard_map/slice | solution.py:481
  320.4 5.2 %copy.59 = bf16[512,1,896]{0,2,1:T(8,128)(2,1)} copy(bf16[512,1,896]{2,1,0:T(2,128)(2,1)} %get-tuple-element.39) | data formatting | bytes 1835008 | tf_op jit(solution)/shard_map/slice | solution.py:481
  325.6 5.2 %copy.53 = bf16[512,1,896]{0,2,1:T(8,128)(2,1)} copy(bf16[512,1,896]{2,1,0:T(2,128)(2,1)} %get-tuple-element.40) | data formatting | bytes 1835008 | tf_op jit(solution)/shard_map/slice | solution.py:499
  330.9 6.5 %fusion.26 = (bf16[512,1,896]{2,1,0:T(2,128)(2,1)}, bf16[512,1,896]{2,1,0:T(2,128)(2,1)S(1)}) fusion(bf16[512,2,896]{2,1,0:T(2,128)(2,1)} %collective-permute-done), kind=kLoop, calls=%fused_computation.64 | loop fusion | bytes 3670016 | tf_op jit(solution)/shard_map/slice | solution.py:481
  337.4 5.2 %copy.58 = bf16[512,1,896]{0,2,1:T(8,128)(2,1)} copy(bf16[512,1,896]{2,1,0:T(2,128)(2,1)} %get-tuple-element.41) | data formatting | bytes 1835008 | tf_op jit(solution)/shard_map/slice | solution.py:481
  342.6 3.9 copy.52
  353.3 3.0 fusion.4
  356.3 3.1 fusion.6
  359.3 3.0 fusion.8
  362.4 2.9 fusion.10
  365.3 8.7 %fusion = f32[4,512]{1,0:T(4,128)S(1)} fusion(f32[4,512,2560]{1,2,0:T(8,128)} %get-tuple-element.34, f32[4,512]{1,0:T(4,128)S(1)} %maximum_maximum_fusion), kind=kLoop, calls=%fused_computation.3 | loop fusion | flops 10483712 | bytes 20987904 | tf_op jit(solution)/shard_map/reduce_sum | solution.py:504
  374.1 9.2 %fusion.12 = bf16[4,224,512]{2,1,0:T(8,128)(2,1)S(1)} fusion(bf16[2560,4,224]{0,2,1:T(8,128)(2,1)S(1)} %bitcast.83, f32[4,512,2560]{1,2,0:T(8,128)} %get-tuple-element.34, f32[4,512]{1,0:T(4,128)S(1)} %fusion, f32[4,512]{1,0:T(4,128)S(1)} %maximum_maximum_fusion), kind=kOutput, calls=%fused_computation.20 | convolution fusion | flops 2364997632 | bytes 26492928 | tf_op jit(solution)/shard_map/hqk,khd->qhd/dot_general | solution.py:505
  385.6 34.0 %tail.1 = (f32[16,128]{1,0:T(8,128)}, f32[8,128]{1,0:T(8,128)}) custom-call(bf16[16,896]{1,0:T(8,128)(2,1)} %convolution_convert_fusion.picked_ref, bf16[896,3584]{1,0:T(8,128)(2,1)} %o_ref.1, f32[1,3584]{1,0:T(1,128)} %reshape.411.gain_ref, bf16[250,3584]{1,0:T(8,128)(2,1)} %un_ref.1), custom_call_target="tpu_custom_call" | custom-call | tf_op jit(solution)/shard_map/tail/pallas_call | solution.py:171
  (70 shorter events, 24.4 us)
Async XLA Ops:
  0.6 111.5 %copy-start.11 = (s32[64]{0:T(128)S(1)}, s32[64]{0:T(128)}, u32[]{:S(2)}) copy-start(s32[64]{0:T(128)} %param.29) | copy-start | bytes 772
  98.3 180.5 %collective-permute-start.3 = (bf16[512,2,896]{2,1,0:T(2,128)(2,1)S(1)}, bf16[512,2,896]{2,1,0:T(2,128)(2,1)}, u32[]{:S(2)}, u32[]{:S(2)}) collective-permute-start(bf16[512,2,896]{2,1,0:T(2,128)(2,1)S(1)} %reshape.407), channel_id=1, source_target_pairs={{0,16},{4,20},{8,24},{12,28},{16,32},{20,36},{24,40},{28,44},{32,4... | collective-permute-start | bytes 5505032 | tf_op jit(solution)/shard_map/ppermute | solution.py:20
  104.2 191.5 %collective-permute-start.2 = (bf16[512,2,896]{2,1,0:T(2,128)(2,1)S(1)}, bf16[512,2,896]{2,1,0:T(2,128)(2,1)}, u32[]{:S(2)}, u32[]{:S(2)}) collective-permute-start(bf16[512,2,896]{2,1,0:T(2,128)(2,1)S(1)} %reshape.407), channel_id=1, source_target_pairs={{0,12},{4,16},{8,20},{12,24},{16,28},{20,32},{24,36},{28,40},{32,4... | collective-permute-start | bytes 5505032 | tf_op jit(solution)/shard_map/ppermute | solution.py:20
  106.8 206.5 %collective-permute-start.1 = (bf16[512,2,896]{2,1,0:T(2,128)(2,1)S(1)}, bf16[512,2,896]{2,1,0:T(2,128)(2,1)}, u32[]{:S(2)}, u32[]{:S(2)}) collective-permute-start(bf16[512,2,896]{2,1,0:T(2,128)(2,1)S(1)} %reshape.407), channel_id=1, source_target_pairs={{0,8},{4,12},{8,16},{12,20},{16,24},{20,28},{24,32},{28,36},{32,40... | collective-permute-start | bytes 5505032 | tf_op jit(solution)/shard_map/ppermute | solution.py:20
  110.2 220.7 %collective-permute-start = (bf16[512,2,896]{2,1,0:T(2,128)(2,1)S(1)}, bf16[512,2,896]{2,1,0:T(2,128)(2,1)}, u32[]{:S(2)}, u32[]{:S(2)}) collective-permute-start(bf16[512,2,896]{2,1,0:T(2,128)(2,1)S(1)} %reshape.407), channel_id=1, source_target_pairs={{0,4},{4,8},{8,12},{12,16},{16,20},{20,24},{24,28},{28,32},{32,36}... | collective-permute-start | bytes 5505032 | tf_op jit(solution)/shard_map/ppermute | solution.py:20
  123.7 150.9 %all-to-all-start = ((bf16[64,8,2,896]{3,1,2,0:T(8,128)(2,1)}), bf16[64,8,2,896]{3,1,2,0:T(8,128)(2,1)}, u32[]{:S(2)}, u32[]{:S(2)}) async-start(bf16[64,8,2,896]{3,1,2,0:T(8,128)(2,1)} %scatter_fusion), calls=%async_computation | async-start | bytes 3670016 | tf_op jit(solution)/shard_map/all_to_all | solution.py:517
  129.8 4.5 %copy-start.12 = (s32[12]{0:T(128)S(1)}, s32[12]{0:T(128)}, u32[]{:S(2)}) copy-start(s32[12]{0:T(128)} %param.27) | copy-start | bytes 148
  129.9 10.8 %copy-start.8 = (s32[512]{0:T(512)}, s32[512]{0:T(512)S(1)}, u32[]{:S(2)}) copy-start(s32[512]{0:T(512)S(1)} %get-tuple-element.53) | copy-start | bytes 6148
  129.9 6.4 %copy-start.9 = (s32[512]{0:T(512)}, s32[512]{0:T(512)S(1)}, u32[]{:S(2)}) copy-start(s32[512]{0:T(512)S(1)} %get-tuple-element.51) | copy-start | bytes 6148
  144.4 12.6 %copy-start.1 = (bf16[512,896]{0,1:T(8,128)(2,1)}, bf16[512,896]{0,1:T(8,128)(2,1)S(1)}, u32[]{:S(2)}) copy-start(bf16[512,896]{0,1:T(8,128)(2,1)S(1)} %copy.57) | copy-start | bytes 2752516
  152.8 4.2 copy-start.13
  152.8 4.2 copy-start.14
  152.8 4.4 %copy-start.10 = (f32[3584]{0:T(1024)S(1)}, f32[3584]{0:T(1024)}, u32[]{:S(2)}) copy-start(f32[3584]{0:T(1024)} %param.25) | copy-start | bytes 43012
  346.5 4.7 %copy-start = (bf16[512,1,896]{0,2,1:T(8,128)(2,1)S(1)}, bf16[512,1,896]{0,2,1:T(8,128)(2,1)}, u32[]{:S(2)}) copy-start(bf16[512,1,896]{0,2,1:T(8,128)(2,1)} %copy.54) | copy-start | bytes 2752516
  346.5 6.8 %copy-start.2 = (bf16[512,896]{0,1:T(8,128)(2,1)S(1)}, bf16[512,896]{0,1:T(8,128)(2,1)}, u32[]{:S(2)}) copy-start(bf16[512,896]{0,1:T(8,128)(2,1)} %copy-done.1) | copy-start | bytes 2752516
  346.5 6.8 %copy-start.6 = (bf16[512,1,896]{0,2,1:T(8,128)(2,1)S(1)}, bf16[512,1,896]{0,2,1:T(8,128)(2,1)}, u32[]{:S(2)}) copy-start(bf16[512,1,896]{0,2,1:T(8,128)(2,1)} %copy.58) | copy-start | bytes 2752516
  346.5 6.8 %copy-start.7 = (pred[512,512]{0,1:T(8,128)(4,1)S(1)}, pred[512,512]{0,1:T(8,128)(4,1)}, u32[]{:S(2)}) copy-start(pred[512,512]{0,1:T(8,128)(4,1)} %get-tuple-element.48) | copy-start | bytes 786436
  353.3 3.0 copy-start.5
  356.3 3.1 copy-start.4
  359.3 3.0 copy-start.3
  362.4 11.7 %slice-start = ((s8[4587520]{0:T(1024)(128)(4,1)}), s8[4194304]{0:T(1024)(128)(4,1)S(1)}, s32[]{:S(2)}) async-start(s8[4587520]{0:T(1024)(128)(4,1)} %bitcast.82), calls=%async_computation.1 | async-start | bytes 8388608
  365.3 8.8 %slice-start.1 = ((s8[4587520]{0:T(1024)(128)(4,1)}), s8[393216]{0:T(1024)(128)(4,1)S(1)}, s32[]{:S(2)}) async-start(s8[4587520]{0:T(1024)(128)(4,1)} %bitcast.82), calls=%async_computation.2 | async-start | bytes 786432

commit v2 on v1

--- a/solution.py
+++ b/solution.py
@@ -12,17 +12,6 @@
 LOOKBACK = 4
 NPROMPT = 12
 RING = 4
-
-
-def passed_along(value, axis, steps):
-    count = lax.axis_size(axis)
-    leading, last = (max(0, -steps), min(count, count - steps))
-    return lax.ppermute(value, axis, [(source, source + steps) for source in range(leading, last)])
-
-
-def segment_of(positions, bounds):
-    counted = jnp.sum((bounds[None, :] <= positions[:, None]).astype(jnp.int32), axis=1)
-    return jnp.where(positions < 0, -1, counted)
 
 
 MESH = pl.DeviceIdType.MESH
@@ -441,6 +430,356 @@
     )
 
 
+def attend_kernel(
+    ring,
+    back,
+    lengths_ref,
+    request_ref,
+    owner_ref,
+    query_ref,
+    kv_ref,
+    out_ref,
+    pages_ref,
+    picked_ref,
+    held,
+    passing,
+    outgoing,
+    keys,
+    values,
+    query,
+    mixed,
+    top,
+    weight,
+    first_key,
+    ahead_send,
+    ahead_recv,
+    back_send,
+    back_recv,
+    late_send,
+    late_recv,
+    sib_send,
+    sib_recv,
+    page_send,
+    page_recv,
+    local_sem,
+):
+    core, z, y = place(ring)
+    chips = ring * ring
+    chip = y * ring + z
+    me = chip * 2 + core
+    rows, double = kv_ref.shape
+    width = double // 2
+    heads = query.shape[0]
+    size = width // heads
+    load = pltpu.make_async_copy(kv_ref, held.at[0], local_sem.at[0])
+    load.start()
+    count = 2 * chips
+    barrier = pltpu.get_barrier_semaphore()
+
+    @pl.loop(1, count)
+    def _(d):
+        pl.semaphore_signal(
+            barrier, inc=1, device_id={"seq": (me + d) % count}, device_id_type=MESH
+        )
+
+    pl.semaphore_wait(barrier, count - 1)
+    load.wait()
+    near = back[0][0]
+
+    def remote(source, target, sent, got, device):
+        return pltpu.make_async_remote_copy(
+            src_ref=source,
+            dst_ref=target,
+            send_sem=sent,
+            recv_sem=got,
+            device_id={"seq": device},
+            device_id_type=MESH,
+        )
+
+    next_chip = ((chip + 1) % chips) * 2 + core
+    behind = (y * ring + (z + ring - 1) % ring) * 2 + core
+    beyond = ((y * ring + (z + 1) % ring + 2) % chips) * 2 + core
+    sibling = chip * 2 + 1 - core
+    spans = ((0, near), (near, rows))
+
+    def ahead(n):
+        part = pl.ds(spans[n][0], spans[n][1] - spans[n][0])
+        return remote(
+            held.at[0, part], held.at[2, part], ahead_send.at[n], ahead_recv.at[n], next_chip
+        )
+
+    def backward(n):
+        start, stop = back[n]
+        return remote(
+            held.at[0, pl.ds(start, stop - start)],
+            passing.at[pl.ds(start - near, stop - start)],
+            back_send.at[n],
+            back_recv.at[n],
+            behind,
+        )
+
+    def relay_ahead():
+        part = pl.ds(0, near)
+        return remote(
+            held.at[2, part], held.at[4, part], late_send.at[0], late_recv.at[0], next_chip
+        )
+
+    def relay_back(n):
+        start, stop = back[n]
+        return remote(
+            passing.at[pl.ds(start - near, stop - start)],
+            held.at[4, pl.ds(start, stop - start)],
+            late_send.at[1 + n],
+            late_recv.at[1 + n],
+            beyond,
+        )
+
+    def beside(n):
+        return remote(
+            held.at[2 * n + 2 * core],
+            held.at[2 * n + 1],
+            sib_send.at[n],
+            sib_recv.at[n],
+            sibling,
+        )
+
+    per = rows // count
+
+    def page_copy(d):
+        owner = (me + d) % count
+        return remote(
+            outgoing.at[pl.ds(pl.multiple_of(owner * per, per), per)],
+            pages_ref.at[pl.ds(pl.multiple_of(me * per, per), per)],
+            page_send.at[d],
+            page_recv.at[d],
+            owner,
+        )
+
+    for n in range(2):
+        ahead(n).start()
+    for n in range(len(back)):
+        backward(n).start()
+
+    @pl.when(core == 0)
+    def _():
+        beside(0).start()
+
+    bounds = []
+    running = 0
+    for k in range(NPROMPT):
+        running = running + lengths_ref[k]
+        bounds.append(running)
+    first_row = me * rows
+    query_pos = first_row + lax.broadcasted_iota(jnp.int32, (rows, 1), 0)
+    start_of = jnp.zeros((rows, 1), jnp.int32)
+    for k in range(NPROMPT):
+        start_of = jnp.where(query_pos >= bounds[k], bounds[k], start_of)
+    first_key[...] = start_of
+    for h in range(heads):
+        query[h] = query_ref[:, h * size : (h + 1) * size]
+    mixed[...] = jnp.zeros_like(mixed)
+    top[...] = jnp.full_like(top, -1e30)
+    weight[...] = jnp.zeros_like(weight)
+    factor = 1.4426950408889634 / size**0.5
+    tile = min(rows, 256)
+
+    def order_pages():
+        pages = owner_ref.shape[1]
+        length = rows // pages
+        square = (pages, pages)
+        down = lax.broadcasted_iota(jnp.int32, square, 0)
+        along = lax.broadcasted_iota(jnp.int32, square, 1)
+        owner_row = jnp.broadcast_to(owner_ref[...], square).astype(jnp.float32)
+        owner_col = jnp.sum(
+            jnp.where(down == along, owner_row, 0.0), axis=1, keepdims=True
+        )
+        same = (owner_col == owner_row) & (down < along)
+        earlier = jnp.sum(jnp.where(same, 1.0, 0.0), axis=0, keepdims=True)
+        target = owner_row[0:1] * (pages // count) + earlier
+        moves = jnp.where(down.astype(jnp.float32) == target, 1.0, 0.0).astype(jnp.bfloat16)
+        spread = jnp.where(
+            lax.broadcasted_iota(jnp.int32, (rows, pages), 0) // length
+            == lax.broadcasted_iota(jnp.int32, (rows, pages), 1),
+            1.0,
+            0.0,
+        ).astype(jnp.bfloat16)
+        tall = jnp.dot(spread, moves, preferred_element_type=jnp.float32).astype(jnp.bfloat16)
+        wide = lax.dot_general(
+            tall, spread, (((1,), (1,)), ((), ())), preferred_element_type=jnp.float32
+        )
+        full = (rows, rows)
+        aligned = (
+            lax.broadcasted_iota(jnp.int32, full, 0) % length
+            == lax.broadcasted_iota(jnp.int32, full, 1) % length
+        )
+        mover = jnp.where(aligned, wide, 0.0).astype(jnp.bfloat16)
+        strip = min(256, double)
+        for c in range(double // strip):
+            cols = slice(c * strip, (c + 1) * strip)
+            outgoing[:, cols] = jnp.dot(
+                mover, held[0, :, cols], preferred_element_type=jnp.float32
+            ).astype(jnp.bfloat16)
+
+    @pl.loop(0, LOOKBACK + 1)
+    def _(t):
+        @pl.when(t == 1)
+        def _():
+            order_pages()
+            ahead(0).wait_recv()
+            relay_ahead().start()
+            for n in range(len(back)):
+                backward(n).wait_recv()
+                relay_back(n).start()
+
+            @pl.loop(1, count)
+            def _(d):
+                page_copy(d).start()
+
+            mine = pl.ds(pl.multiple_of(me * per, per), per)
+            pltpu.make_async_copy(outgoing.at[mine], pages_ref.at[mine], local_sem.at[1]).start()
+            ahead(1).wait_recv()
+
+            @pl.when(core == 1)
+            def _():
+                beside(0).start()
+
+            @pl.when(core == 0)
+            def _():
+                beside(1).start()
+
+        @pl.when(t == 2)
+        def _():
+            beside(0).wait_recv()
+
+        @pl.when(t == 3)
+        def _():
+            relay_ahead().wait_recv()
+            for n in range(len(back)):
+                relay_back(n).wait_recv()
+
+            @pl.when(core == 1)
+            def _():
+                beside(1).start()
+
+        @pl.when(t == 4)
+        def _():
+            beside(1).wait_recv()
+
+        offset = 0
+        for n, value in enumerate((0, 2, 1, 4, 3)):
+            offset = offset + jnp.where(t == n, value, 0)
+        key_pos = (me - offset) * rows + lax.broadcasted_iota(jnp.int32, (1, rows), 1)
+        for h in range(heads):
+            keys[...] = held[offset, :, h * size : (h + 1) * size]
+            values[...] = held[offset, :, width + h * size : width + (h + 1) * size]
+
+            @pl.loop(0, rows // tile)
+            def _(b, h=h):
+                part = pl.ds(pl.multiple_of(b * tile, tile), tile)
+                raw = lax.dot_general(
+                    query[h, part, :],
+                    keys[...],
+                    (((1,), (1,)), ((), ())),
+                    preferred_element_type=jnp.float32,
+                )
+                here = first_row + b * tile + lax.broadcasted_iota(jnp.int32, (tile, 1), 0)
+                visible = (key_pos >= first_key[part, :]) & (key_pos <= here)
+                scores = jnp.where(visible, raw * factor, -1e30)
+                old = top[h, part, :]
+                new = jnp.maximum(old, jnp.max(scores, axis=1, keepdims=True))
+                terms = jnp.exp2(scores - new)
+                shrink = jnp.exp2(old - new)
+                weight[h, part, :] = weight[h, part, :] * shrink + jnp.sum(
+                    terms, axis=1, keepdims=True
+                )
+                mixed[h, part, :] = mixed[h, part, :] * shrink + jnp.dot(
+                    terms.astype(jnp.bfloat16), values[...], preferred_element_type=jnp.float32
+                )
+                top[h, part, :] = new
+
+    for h in range(heads):
+        out_ref[:, h * size : (h + 1) * size] = (mixed[h] / weight[h]).astype(jnp.bfloat16)
+    requests = picked_ref.shape[0]
+    which = lax.broadcasted_iota(jnp.int32, (requests, 1), 0)
+    last = jnp.zeros((requests, 1), jnp.int32)
+    for r in range(requests):
+        end = 0
+        for k in range(NPROMPT):
+            end = end + jnp.where(request_ref[r] == k, bounds[k], 0)
+        last = jnp.where(which == r, end - 1, last)
+    chosen = jnp.where(
+        last == first_row + lax.broadcasted_iota(jnp.int32, (requests, rows), 1), 1.0, 0.0
+    ).astype(jnp.bfloat16)
+    picked_ref[...] = jnp.dot(
+        chosen, out_ref[...], preferred_element_type=jnp.float32
+    ).astype(jnp.bfloat16)
+
+    for n in range(2):
+        ahead(n).wait_send()
+        beside(n).wait_send()
+    relay_ahead().wait_send()
+    for n in range(len(back)):
+        backward(n).wait_send()
+        relay_back(n).wait_send()
+
+    @pl.loop(1, count)
+    def _(d):
+        page_copy(d).wait()
+
+    mine = pl.ds(pl.multiple_of(me * per, per), per)
+    pltpu.make_async_copy(outgoing.at[mine], pages_ref.at[mine], local_sem.at[1]).wait()
+
+
+def attend(lengths, req_prompt, page_owner, queries, local_rows, ring):
+    rows, width = queries.shape
+    heads = width // HEAD
+    count = 2 * ring * ring
+    near = rows * 11 // 32
+    third = (rows - near) // 3
+    back = tuple((near + n * third, near + (n + 1) * third) for n in range(3))
+    vmem = pl.BlockSpec(memory_space=pltpu.VMEM)
+    smem = pl.BlockSpec(memory_space=pltpu.SMEM)
+    anywhere = pl.BlockSpec(memory_space=pl.ANY)
+    dma = pltpu.SemaphoreType.DMA
+    return pl.pallas_call(
+        functools.partial(attend_kernel, ring, back),
+        out_shape=(
+            jax.ShapeDtypeStruct((rows, width), jnp.bfloat16),
+            jax.ShapeDtypeStruct((rows, 2 * width), jnp.bfloat16),
+            jax.ShapeDtypeStruct((req_prompt.shape[0], width), jnp.bfloat16),
+        ),
+        in_specs=[smem, smem, vmem, vmem, anywhere],
+        out_specs=(vmem, anywhere, vmem),
+        scratch_shapes=[
+            pltpu.VMEM((LOOKBACK + 1, rows, 2 * width), jnp.bfloat16),
+            pltpu.VMEM((rows - near, 2 * width), jnp.bfloat16),
+            pltpu.VMEM((rows, 2 * width), jnp.bfloat16),
+            pltpu.VMEM((rows, HEAD), jnp.bfloat16),
+            pltpu.VMEM((rows, HEAD), jnp.bfloat16),
+            pltpu.VMEM((heads, rows, HEAD), jnp.bfloat16),
+            pltpu.VMEM((heads, rows, HEAD), jnp.float32),
+            pltpu.VMEM((heads, rows, 1), jnp.float32),
+            pltpu.VMEM((heads, rows, 1), jnp.float32),
+            pltpu.VMEM((rows, 1), jnp.int32),
+            dma((2,)),
+            dma((2,)),
+            dma((3,)),
+            dma((3,)),
+            dma((4,)),
+            dma((4,)),
+            dma((2,)),
+            dma((2,)),
+            dma((count,)),
+            dma((count,)),
+            dma((2,)),
+        ],
+        compiler_params=pltpu.CompilerParams(
+            collective_id=2, has_side_effects=True, vmem_limit_bytes=60 << 20
+        ),
+        name="attend",
+    )(lengths, req_prompt, page_owner.reshape(1, -1), queries, local_rows)
+
+
 def local(
     hidden_cat,
     norm_gain,
@@ -458,74 +797,12 @@
     req_prompt,
     page_owner,
 ):
-    rows_here = hidden_cat.shape[0]
-    width = k_weight.shape[1]
-    heads_here = width // HEAD
-    seq_count = lax.axis_size("seq")
     local_rows = project(
         hidden_cat, norm_gain, k_weight, v_weight, k_down, v_down, k_up, v_up, RING
     )
-    local_kv = local_rows.reshape(rows_here, 2, width)
-    kv_blocks = [local_kv]
-    for offset in range(1, LOOKBACK + 1):
-        kv_blocks.append(passed_along(local_kv, "seq", offset))
-    bounds = jnp.cumsum(lengths)
-    first_row = lax.axis_index("seq") * rows_here
-    query_pos = first_row + jnp.arange(rows_here, dtype=jnp.int32)
-    query_seg = segment_of(query_pos, bounds)
-    query_heads = queries.reshape(rows_here, heads_here, HEAD)
-    scale = 1.0 / HEAD**0.5
-    score_list = []
-    value_list = []
-    for offset in range(LOOKBACK + 1):
-        key_block = kv_blocks[offset][:, 0].reshape(rows_here, heads_here, HEAD)
-        key_pos = query_pos - offset * rows_here
-        key_seg = segment_of(key_pos, bounds)
-        visible = (query_seg[:, None] == key_seg[None, :]) & (
-            key_pos[None, :] <= query_pos[:, None]
-        )
-
-        def compute_scores(key_block=key_block, visible=visible):
-            raw = (
-                jnp.einsum(
-                    "qhd,khd->hqk", query_heads, key_block, preferred_element_type=jnp.float32
-                )
-                * scale
-            )
-            return jnp.where(visible[None], raw, -1e30)
-
-        blocked = compute_scores()
-        score_list.append(blocked)
-        value_list.append(kv_blocks[offset][:, 1].reshape(rows_here, heads_here, HEAD))
-    scores = jnp.concatenate(score_list, axis=2)
-    value_all = jnp.concatenate(value_list, axis=0)
-    row_max = jnp.max(scores, axis=2, keepdims=True)
-    expo_terms = jnp.exp(scores - row_max)
-    probs = (expo_terms / jnp.sum(expo_terms, axis=2, keepdims=True)).astype(jnp.bfloat16)
-    mixed = jnp.einsum("hqk,khd->qhd", probs, value_all, preferred_element_type=jnp.float32)
-    attended = mixed.reshape(rows_here, width).astype(jnp.bfloat16)
-    pages_here = rows_here // PAGE
-    per_owner = pages_here // seq_count
-    onehot = (page_owner[:, None] == jnp.arange(seq_count, dtype=jnp.int32)[None, :]).astype(
-        jnp.int32
-    )
-    before = jnp.cumsum(onehot, axis=0) - onehot
-    earlier = jnp.sum(before * onehot, axis=1)
-    target = page_owner * per_owner + earlier
-    pages = local_kv.reshape(pages_here, PAGE, 2, width)
-    outgoing = jnp.zeros_like(pages).at[target].set(pages)
-    kv_cache = lax.all_to_all(outgoing, "seq", split_axis=0, concat_axis=0, tiled=True)
-    last_pos = bounds - 1
-    request_pos = jnp.sum(
-        jnp.where(
-            req_prompt[:, None] == jnp.arange(NPROMPT, dtype=jnp.int32)[None, :],
-            last_pos[None, :],
-            0,
-        ),
-        axis=1,
-    )
-    selector = (request_pos[:, None] == query_pos[None, :]).astype(jnp.bfloat16)
-    picked = jnp.dot(selector, attended, preferred_element_type=jnp.float32).astype(jnp.bfloat16)
+    attended, pages, picked = attend(lengths, req_prompt, page_owner, queries, local_rows, RING)
+    rows, width = attended.shape
+    kv_cache = pages.reshape(rows // PAGE, PAGE, 2, width)
     state_norm, logit_max = tail(
         picked, o_weight, final_gain, unembed, RING, RING, lax.axis_size("tp")
     )

time: 425 us -> 244 us (0.57)
  waiting for transfers between devices: 117 us -> 0 us
  local copies, waits for them, and re-layouts: 115 us -> 6.75 us
  Pallas kernels: 128 us -> 234 us
  matrix products: 26.4 us -> 0 us
  starting transfers between devices: 19.9 us -> 0 us
  other arithmetic: 15.4 us -> 0 us
    all_to_all x1 -> x0, waiting for transfers between devices: 117 us -> none  [local(): lax.all_to_all(outgoing, 'seq', split_axis=0, concat_axis=0, tiled=True)]
    pallas_call x0 -> x1, Pallas kernels: none -> 102 us  [attend(): pl.pallas_call(functools.partial(attend_kernel, ring, back), out_shape=(j...]
    slice x15 -> x0, local copies, waits for them, and re-layouts: 81.8 us -> none  [the longest x10 58.6 us: local(): key_block = kv_blocks[offset][:, 0].reshape(rows_here, heads_here, HEAD)]
    dot_general x7 -> x0, matrix products: 26.4 us -> none  [the longest x5 16.2 us: compute_scores(): jnp.einsum('qhd,khd->hqk', query_heads, key_block, preferred_element_type...]
    ppermute x4 -> x0, starting transfers between devices: 13.8 us -> none  [passed_along(): lax.ppermute(value, axis, [(source, source + steps) for source in range(l...]
    unnamed x41 -> x8, local copies, waits for them, and re-layouts: 13.7 us -> 3.62 us
    scatter x1 -> x0, local copies, waits for them, and re-layouts: 9.85 us -> none  [local(): outgoing = jnp.zeros_like(pages).at[target].set(pages)]
    reduce_sum x4 -> x0, other arithmetic: 9.21 us -> none  [the longest x1 8.73 us: local(): jnp.sum(expo_terms, axis=2, keepdims=True)]
  transfers between devices with their start and end apart: 5 -> 0, of which waited for: 1 -> 0; matrix products, arithmetic and copies ran while one was open for 23% -> 0% of each run, Pallas kernels for 0% -> 0%
where the time goes in v2:
time: 244 us; the launch traced here: 242 us
  Pallas kernels  234 us (96%)
  local copies, waits for them, and re-layouts  6.75 us (3%)
    pallas_call x1, Pallas kernels, attend(): pl.pallas_call(functools.partial(attend_kernel, ring, back), out_shape=(j...  102 us
    pallas_call x1, Pallas kernels, project(): pl.pallas_call(functools.partial(project_kernel, ring), out_shape=jax.Sha...  93.8 us
    pallas_call x1, Pallas kernels, tail(): pl.pallas_call(functools.partial(tail_kernel, zs, ys, tps), out_shape=(ja...  38.7 us

profile of v2, /device:TPU:1, one launch (start us, length us, event | category | flops | bytes accessed | tf_op | source)
XLA Modules:
  0.0 241.9 jit_solution(6520696438978115307)
XLA Ops:
  0.6 93.8 %project.1.kv_ref = bf16[512,1792]{1,0:T(8,128)(2,1)} custom-call(bf16[512,7168]{1,0:T(8,128)(2,1)} %hidden_ref.1, f32[1,7168]{1,0:T(1,128)} %bitcast.6, bf16[224,896]{1,0:T(8,128)(2,1)} %kw_ref.1, bf16[224,896]{1,0:T(8,128)(2,1)} %vw_ref.1, bf16[224,128]{1,0:T(8,128)(2,1)} %kd_ref.1, bf16[224,128]{1,0:T(8,128)(2,1)} %vd_ref.1, bf16[128,896]{1,0:T(8,128)(2,1)} %ku_ref.1, ...), custom_call_target="tpu_custom_call" | custom-call | tf_op jit(solution)/shard_map/project/pallas_call | solution.py:402
  94.5 0.0 copy-start.2
  94.5 102.0 %attend.1 = (bf16[512,896]{1,0:T(8,128)(2,1)}, bf16[512,1792]{1,0:T(8,128)(2,1)}, bf16[16,896]{1,0:T(8,128)(2,1)}) custom-call(s32[12]{0:T(128)} %lengths_ref.1, s32[16]{0:T(128)} %request_ref.1, s32[1,64]{1,0:T(1,128)} %bitcast.7, bf16[512,896]{1,0:T(8,128)(2,1)} %query_ref.1, bf16[512,1792]{1,0:T(8,128)(2,1)} %project.1.kv_ref), custom_call_target="tpu_custom_call" | custom-call | tf_op jit(solution)/shard_map/attend/pallas_call | solution.py:744
  196.4 0.0 copy-done.2
  196.4 0.6 reshape.23.gain_ref
  197.1 0.0 copy-start
  197.1 38.7 %tail.1 = (f32[16,128]{1,0:T(8,128)}, f32[8,128]{1,0:T(8,128)}) custom-call(bf16[16,896]{1,0:T(8,128)(2,1)} %get-tuple-element.11.picked_ref, bf16[896,3584]{1,0:T(8,128)(2,1)} %o_ref.1, f32[1,3584]{1,0:T(1,128)} %reshape.23.gain_ref, bf16[250,3584]{1,0:T(8,128)(2,1)} %un_ref.1), custom_call_target="tpu_custom_call" | custom-call | tf_op jit(solution)/shard_map/tail/pallas_call | solution.py:160
  235.8 1.2 slice_bitcast_fusion
  237.0 1.3 slice_reduce_fusion
  238.3 0.0 copy-done
  238.3 0.0 copy-start.1
  238.3 2.7 %copy.20 = bf16[64,8,2,896]{3,2,1,0:T(2,128)(2,1)} copy(bf16[64,8,2,896]{3,1,2,0:T(8,128)(2,1)S(1)} %bitcast.5) | data formatting | bytes 3670016
  241.0 0.0 copy-done.1
  241.0 0.9 copy.22
Async XLA Ops:
  94.5 102.0 %copy-start.2 = (f32[3584]{0:T(1024)S(1)}, f32[3584]{0:T(1024)}, u32[]{:S(2)}) copy-start(f32[3584]{0:T(1024)} %param.25) | copy-start | bytes 43012
  197.1 41.2 %copy-start = (bf16[512,1792]{1,0:T(8,128)(2,1)S(1)}, bf16[512,1792]{1,0:T(8,128)(2,1)}, u32[]{:S(2)}) copy-start(bf16[512,1792]{1,0:T(8,128)(2,1)} %get-tuple-element.10) | copy-start | bytes 5505028
  238.3 2.7 %copy-start.1 = (bf16[512,896]{1,0:T(8,128)(2,1)S(1)}, bf16[512,896]{1,0:T(8,128)(2,1)}, u32[]{:S(2)}) copy-start(bf16[512,896]{1,0:T(8,128)(2,1)} %get-tuple-element.26) | copy-start | bytes 2752516

commit v3 on v2

--- a/solution.py
+++ b/solution.py
@@ -35,23 +35,19 @@
     pl.semaphore_wait(barrier, len(peers))
 
 
-def tail_kernel(
-    zs,
-    ys,
+def last_tokens(
+    ring,
     tps,
-    picked_ref,
-    o_ref,
+    fill,
+    picked,
+    o_buf,
     gain_ref,
-    un_ref,
+    un_buf,
     norm_ref,
     max_ref,
-    o_buf,
-    un_buf,
-    row_c,
-    row_z,
-    row_y,
-    sum_c,
-    sum_z,
+    row_a,
+    row_b,
+    row_sum,
     parts,
     states,
     final_buf,
@@ -59,23 +55,28 @@
     max_got,
     send,
     recv,
-    local_sem,
+    load_o,
+    load_u,
 ):
-    core, z, y = place(zs)
+    core, z, y = place(ring)
     x = lax.axis_index("tp")
-    rows, width = picked_ref.shape
+    rows, width = picked.shape
     chunk = o_buf.shape[1]
-    load_o = pltpu.make_async_copy(
-        o_ref.at[:, pl.ds(pl.multiple_of(z * chunk, chunk), chunk)], o_buf, local_sem.at[0]
-    )
-    load_o.start()
-    load_u = pltpu.make_async_copy(un_ref, un_buf, local_sem.at[1])
-    load_u.start()
-    on_core = [{"seq": seq_id(1 - core, z, y, zs)}]
-    on_z = [{"seq": seq_id(core, (z + k) % zs, y, zs)} for k in range(1, zs)]
-    on_y = [{"seq": seq_id(core, z, (y + k) % ys, zs)} for k in range(1, ys)]
+    near = [
+        {"seq": seq_id((core + c) % 2, (z + k) % ring, y, ring)}
+        for k in range(ring)
+        for c in range(2)
+        if k + c > 0
+    ]
+    on_z = [{"seq": seq_id(core, (z + k) % ring, y, ring)} for k in range(1, ring)]
+    on_y = [{"seq": seq_id(core, z, (y + k) % ring, ring)} for k in range(1, ring)]
     on_x = [{"tp": (x + k) % tps} for k in range(1, tps)]
-    enter(on_core + on_z + on_y + on_x)
+    far = [
+        {"seq": seq_id(core, z, (y + k) % ring, ring), "tp": (x + j) % tps}
+        for k in range(ring)
+        for j in range(tps)
+        if k + j > 0
+    ]
     used = [0]
 
     def exchange(peers, source, target):
@@ -93,44 +94,38 @@
             )
             copy.start()
             copies.append(copy)
-        return copies
-
-    def finish(copies):
+        fill()
         for copy in copies:
             copy.wait()
 
-    going = exchange(on_core, picked_ref, lambda k: row_c.at[k])
-    final_buf[...] = jnp.zeros_like(final_buf)
-    finish(going)
-    sum_c[...] = picked_ref[...] + row_c[0]
-    finish(exchange(on_z, sum_c, lambda k: row_z.at[k]))
-    total = sum_c[...]
-    for k in range(zs - 1):
-        total = total + row_z[k]
-    sum_z[...] = total
-    finish(exchange(on_y, sum_z, lambda k: row_y.at[k]))
-    for k in range(ys - 1):
-        total = total + row_y[k]
+    exchange(near, picked, lambda k: row_a.at[k])
+    total = picked[...]
+    for k in range(len(near)):
+        total = total + row_a[k]
+    row_sum[...] = total
+    exchange(on_y, row_sum, lambda k: row_b.at[k])
+    for k in range(len(on_y)):
+        total = total + row_b[k]
     load_o.wait()
     parts[x] = jnp.dot(total, o_buf[...], preferred_element_type=jnp.float32)
-    finish(exchange(on_x, parts.at[x], lambda k: parts.at[x]))
+    exchange(on_x, parts.at[x], lambda k: parts.at[x])
     state = parts[0]
     for k in range(1, tps):
         state = state + parts[k]
     states[z] = state
-    finish(exchange(on_z, states.at[z], lambda k: states.at[z]))
+    exchange(on_z, states.at[z], lambda k: states.at[z])
     squares = jnp.zeros((rows, 1), jnp.float32)
-    for k in range(zs):
+    for k in range(ring):
         squares = squares + jnp.sum(states[k] * states[k], axis=1, keepdims=True)
     norm_ref[...] = jnp.broadcast_to(jnp.sqrt(squares), norm_ref.shape)
-    inverse = lax.rsqrt(squares / (zs * chunk) + 1e-05)
-    for k in range(zs):
+    inverse = lax.rsqrt(squares / (ring * chunk) + 1e-05)
+    for k in range(ring):
         final_buf[k, 0:rows, :] = (
             states[k] * inverse * gain_ref[:, k * chunk : (k + 1) * chunk]
         ).astype(jnp.bfloat16)
     load_u.wait()
     logits = jnp.zeros((un_buf.shape[0], final_buf.shape[1]), jnp.float32)
-    for k in range(zs):
+    for k in range(ring):
         logits = logits + lax.dot_general(
             un_buf[:, k * chunk : (k + 1) * chunk],
             final_buf[k],
@@ -138,54 +133,14 @@
             preferred_element_type=jnp.float32,
         )
     best = jnp.broadcast_to(jnp.max(logits, axis=0, keepdims=True), max_ref.shape)
-    place_at = 0
-    for step, peers in enumerate((on_core, on_z, on_y, on_x)):
+    start = 0
+    for step, peers in enumerate((near, far)):
         max_own[step] = best
-        start = place_at
-        finish(exchange(peers, max_own.at[step], lambda k: max_got.at[start + k]))
+        exchange(peers, max_own.at[step], lambda k, start=start: max_got.at[start + k])
         for k in range(len(peers)):
             best = jnp.maximum(best, max_got[start + k])
-        place_at = place_at + len(peers)
+        start = start + len(peers)
     max_ref[...] = best
-
-
-def tail(picked, o_weight, final_gain, unembed, zs, ys, tps):
-    rows, width = picked.shape
-    model = o_weight.shape[1]
-    chunk = model // zs
-    pads = 128
-    copies = (1 + zs + ys + tps - 3) * 2 + zs - 1
-    vmem = pl.BlockSpec(memory_space=pltpu.VMEM)
-    anywhere = pl.BlockSpec(memory_space=pl.ANY)
-    norm, best = pl.pallas_call(
-        functools.partial(tail_kernel, zs, ys, tps),
-        out_shape=(
-            jax.ShapeDtypeStruct((rows, 128), jnp.float32),
-            jax.ShapeDtypeStruct((8, pads), jnp.float32),
-        ),
-        in_specs=[vmem, anywhere, vmem, anywhere],
-        out_specs=(vmem, vmem),
-        scratch_shapes=[
-            pltpu.VMEM((width, chunk), jnp.bfloat16),
-            pltpu.VMEM(unembed.shape, jnp.bfloat16),
-            pltpu.VMEM((1, rows, width), jnp.bfloat16),
-            pltpu.VMEM((max(1, zs - 1), rows, width), jnp.bfloat16),
-            pltpu.VMEM((max(1, ys - 1), rows, width), jnp.bfloat16),
-            pltpu.VMEM((rows, width), jnp.bfloat16),
-            pltpu.VMEM((rows, width), jnp.bfloat16),
-            pltpu.VMEM((tps, rows, chunk), jnp.float32),
-            pltpu.VMEM((zs, rows, chunk), jnp.float32),
-            pltpu.VMEM((zs, pads, chunk), jnp.bfloat16),
-            pltpu.VMEM((4, 8, pads), jnp.float32),
-            pltpu.VMEM((1 + zs + ys + tps - 3, 8, pads), jnp.float32),
-            pltpu.SemaphoreType.DMA((copies,)),
-            pltpu.SemaphoreType.DMA((copies,)),
-            pltpu.SemaphoreType.DMA((2,)),
-        ],
-        compiler_params=pltpu.CompilerParams(collective_id=0, has_side_effects=True),
-        name="tail",
-    )(picked, o_weight, final_gain.reshape(1, model), unembed)
-    return norm[:, 0], best[0, :rows]
 
 
 ORDER = (
@@ -432,15 +387,20 @@
 
 def attend_kernel(
     ring,
+    tps,
     back,
     lengths_ref,
     request_ref,
     owner_ref,
     query_ref,
     kv_ref,
+    o_ref,
+    gain_ref,
+    un_ref,
     out_ref,
     pages_ref,
-    picked_ref,
+    norm_ref,
+    max_ref,
     held,
     passing,
     outgoing,
@@ -462,6 +422,19 @@
     page_send,
     page_recv,
     local_sem,
+    picked_ref,
+    o_buf,
+    un_buf,
+    row_a,
+    row_b,
+    row_sum,
+    parts,
+    states,
+    final_buf,
+    max_own,
+    max_got,
+    tail_send,
+    tail_recv,
 ):
     core, z, y = place(ring)
     chips = ring * ring
@@ -473,7 +446,15 @@
     size = width // heads
     load = pltpu.make_async_copy(kv_ref, held.at[0], local_sem.at[0])
     load.start()
+    chunk = o_buf.shape[1]
+    load_o = pltpu.make_async_copy(
+        o_ref.at[:, pl.ds(pl.multiple_of(z * chunk, chunk), chunk)], o_buf, local_sem.at[2]
+    )
+    load_o.start()
+    load_u = pltpu.make_async_copy(un_ref, un_buf, local_sem.at[3])
+    load_u.start()
     count = 2 * chips
+    x = lax.axis_index("tp")
     barrier = pltpu.get_barrier_semaphore()
 
     @pl.loop(1, count)
@@ -482,7 +463,15 @@
             barrier, inc=1, device_id={"seq": (me + d) % count}, device_id_type=MESH
         )
 
-    pl.semaphore_wait(barrier, count - 1)
+    for k in range(ring):
+        for j in range(1, tps):
+            pl.semaphore_signal(
+                barrier,
+                inc=1,
+                device_id={"seq": seq_id(core, z, (y + k) % ring, ring), "tp": (x + j) % tps},
+                device_id_type=MESH,
+            )
+    pl.semaphore_wait(barrier, count - 1 + ring * (tps - 1))
     load.wait()
     near = back[0][0]
 
@@ -546,14 +535,28 @@
     per = rows // count
 
     def page_copy(d):
-        owner = (me + d) % count
+        down, along, other = d
+        owner = seq_id((core + other) % 2, (z + along) % ring, (y + down) % ring, ring)
+        n = (down * ring + along) * 2 + other
         return remote(
             outgoing.at[pl.ds(pl.multiple_of(owner * per, per), per)],
             pages_ref.at[pl.ds(pl.multiple_of(me * per, per), per)],
-            page_send.at[d],
-            page_recv.at[d],
+            page_send.at[n],
+            page_recv.at[n],
             owner,
         )
+
+    flat = [(k, 0, c) for k in range(ring) for c in range(2) if k + c > 0]
+    batches = [
+        [(k, 1, 0), ((ring - k) % ring, ring - 1, 0), (k, 1, 1), ((ring - k) % ring, ring - 1, 1)]
+        for k in range(ring)
+    ] + [[(k, 2, 0), (k, 2, 1), (k + 2, 2, 0), (k + 2, 2, 1)] for k in range(2)]
+    waiting = list(batches)
+
+    def fill():
+        if waiting:
+            for d in waiting.pop(0):
+                page_copy(d).start()
 
     for n in range(2):
         ahead(n).start()
@@ -631,8 +634,7 @@
                 backward(n).wait_recv()
                 relay_back(n).start()
 
-            @pl.loop(1, count)
-            def _(d):
+            for d in flat:
                 page_copy(d).start()
 
             mine = pl.ds(pl.multiple_of(me * per, per), per)
@@ -661,9 +663,13 @@
             def _():
                 beside(1).start()
 
+            fill()
+            fill()
+
         @pl.when(t == 4)
         def _():
             beside(1).wait_recv()
+            fill()
 
         offset = 0
         for n, value in enumerate((0, 2, 1, 4, 3)):
@@ -713,7 +719,32 @@
     picked_ref[...] = jnp.dot(
         chosen, out_ref[...], preferred_element_type=jnp.float32
     ).astype(jnp.bfloat16)
-
+    final_buf[...] = jnp.zeros_like(final_buf)
+    last_tokens(
+        ring,
+        tps,
+        fill,
+        picked_ref,
+        o_buf,
+        gain_ref,
+        un_buf,
+        norm_ref,
+        max_ref,
+        row_a,
+        row_b,
+        row_sum,
+        parts,
+        states,
+        final_buf,
+        max_own,
+        max_got,
+        tail_send,
+        tail_recv,
+        load_o,
+        load_u,
+    )
+    while waiting:
+        fill()
     for n in range(2):
         ahead(n).wait_send()
         beside(n).wait_send()
@@ -722,34 +753,50 @@
         backward(n).wait_send()
         relay_back(n).wait_send()
 
-    @pl.loop(1, count)
-    def _(d):
-        page_copy(d).wait()
-
+    for batch in [flat] + batches:
+        for d in batch:
+            page_copy(d).wait()
     mine = pl.ds(pl.multiple_of(me * per, per), per)
     pltpu.make_async_copy(outgoing.at[mine], pages_ref.at[mine], local_sem.at[1]).wait()
 
 
-def attend(lengths, req_prompt, page_owner, queries, local_rows, ring):
+def attend(
+    lengths,
+    req_prompt,
+    page_owner,
+    queries,
+    local_rows,
+    o_weight,
+    final_gain,
+    unembed,
+    ring,
+    tps,
+):
     rows, width = queries.shape
     heads = width // HEAD
     count = 2 * ring * ring
     near = rows * 11 // 32
     third = (rows - near) // 3
     back = tuple((near + n * third, near + (n + 1) * third) for n in range(3))
+    requests = req_prompt.shape[0]
+    model = o_weight.shape[1]
+    chunk = model // ring
+    around, far = 2 * ring - 1, ring * tps - 1
+    copies = 2 * around + far + 2 * (ring - 1) + tps - 1
     vmem = pl.BlockSpec(memory_space=pltpu.VMEM)
     smem = pl.BlockSpec(memory_space=pltpu.SMEM)
     anywhere = pl.BlockSpec(memory_space=pl.ANY)
     dma = pltpu.SemaphoreType.DMA
-    return pl.pallas_call(
-        functools.partial(attend_kernel, ring, back),
+    attended, pages, norm, best = pl.pallas_call(
+        functools.partial(attend_kernel, ring, tps, back),
         out_shape=(
             jax.ShapeDtypeStruct((rows, width), jnp.bfloat16),
             jax.ShapeDtypeStruct((rows, 2 * width), jnp.bfloat16),
-            jax.ShapeDtypeStruct((req_prompt.shape[0], width), jnp.bfloat16),
+            jax.ShapeDtypeStruct((requests, 128), jnp.float32),
+            jax.ShapeDtypeStruct((8, 128), jnp.float32),
         ),
-        in_specs=[smem, smem, vmem, vmem, anywhere],
-        out_specs=(vmem, anywhere, vmem),
+        in_specs=[smem, smem, vmem, vmem, anywhere, anywhere, vmem, anywhere],
+        out_specs=(vmem, anywhere, vmem, vmem),
         scratch_shapes=[
             pltpu.VMEM((LOOKBACK + 1, rows, 2 * width), jnp.bfloat16),
             pltpu.VMEM((rows - near, 2 * width), jnp.bfloat16),
@@ -771,13 +818,36 @@
             dma((2,)),
             dma((count,)),
             dma((count,)),
-            dma((2,)),
+            dma((4,)),
+            pltpu.VMEM((requests, width), jnp.bfloat16),
+            pltpu.VMEM((width, chunk), jnp.bfloat16),
+            pltpu.VMEM(unembed.shape, jnp.bfloat16),
+            pltpu.VMEM((around, requests, width), jnp.bfloat16),
+            pltpu.VMEM((ring - 1, requests, width), jnp.bfloat16),
+            pltpu.VMEM((requests, width), jnp.bfloat16),
+            pltpu.VMEM((tps, requests, chunk), jnp.float32),
+            pltpu.VMEM((ring, requests, chunk), jnp.float32),
+            pltpu.VMEM((ring, 128, chunk), jnp.bfloat16),
+            pltpu.VMEM((2, 8, 128), jnp.float32),
+            pltpu.VMEM((around + far, 8, 128), jnp.float32),
+            dma((copies,)),
+            dma((copies,)),
         ],
         compiler_params=pltpu.CompilerParams(
             collective_id=2, has_side_effects=True, vmem_limit_bytes=60 << 20
         ),
         name="attend",
-    )(lengths, req_prompt, page_owner.reshape(1, -1), queries, local_rows)
+    )(
+        lengths,
+        req_prompt,
+        page_owner.reshape(1, -1),
+        queries,
+        local_rows,
+        o_weight,
+        final_gain.reshape(1, model),
+        unembed,
+    )
+    return attended, pages, norm[:, 0], best[0, :requests]
 
 
 def local(
@@ -800,12 +870,20 @@
     local_rows = project(
         hidden_cat, norm_gain, k_weight, v_weight, k_down, v_down, k_up, v_up, RING
     )
-    attended, pages, picked = attend(lengths, req_prompt, page_owner, queries, local_rows, RING)
+    attended, pages, state_norm, logit_max = attend(
+        lengths,
+        req_prompt,
+        page_owner,
+        queries,
+        local_rows,
+        o_weight,
+        final_gain,
+        unembed,
+        RING,
+        lax.axis_size("tp"),
+    )
     rows, width = attended.shape
     kv_cache = pages.reshape(rows // PAGE, PAGE, 2, width)
-    state_norm, logit_max = tail(
-        picked, o_weight, final_gain, unembed, RING, RING, lax.axis_size("tp")
-    )
     return (attended, kv_cache, state_norm, logit_max)
 
 

time: 244 us -> 227 us (0.930)
  Pallas kernels: 234 us -> 218 us
    pallas_call x2 -> x1, Pallas kernels: 141 us -> 124 us  [attend(): pl.pallas_call(functools.partial(attend_kernel, ring, tps, back), out_sha...]
    unnamed x8 -> x6, local copies, waits for them, and re-layouts: 3.62 us -> 5.18 us
where the time goes in v3:
time: 227 us
  Pallas kernels  218 us (96%)
  local copies, waits for them, and re-layouts  8.33 us (4%)
    pallas_call x1, Pallas kernels, attend(): pl.pallas_call(functools.partial(attend_kernel, ring, tps, back), out_sha...  124 us
    pallas_call x1, Pallas kernels, project(): pl.pallas_call(functools.partial(project_kernel, ring), out_shape=jax.Sha...  93.8 us
    unnamed x6, local copies, waits for them, and re-layouts  5.18 us

profile of v3, /device:TPU:1, one launch (start us, length us, event | category | flops | bytes accessed | tf_op | source)
XLA Modules:
  0.0 226.6 jit_solution(11854739357820967993)
XLA Ops:
  0.6 1.3 reshape.22.gain_ref
  2.0 93.8 %project.1.kv_ref = bf16[512,1792]{1,0:T(8,128)(2,1)} custom-call(bf16[512,7168]{1,0:T(8,128)(2,1)} %hidden_ref.1, f32[1,7168]{1,0:T(1,128)} %bitcast.6, bf16[224,896]{1,0:T(8,128)(2,1)} %kw_ref.1, bf16[224,896]{1,0:T(8,128)(2,1)} %vw_ref.1, bf16[224,128]{1,0:T(8,128)(2,1)} %kd_ref.1, bf16[224,128]{1,0:T(8,128)(2,1)} %vd_ref.1, bf16[128,896]{1,0:T(8,128)(2,1)} %ku_ref.1, ...), custom_call_target="tpu_custom_call" | custom-call | tf_op jit(solution)/shard_map/project/pallas_call | solution.py:357
  95.7 123.8 %attend.1 = (bf16[512,896]{1,0:T(8,128)(2,1)}, bf16[512,1792]{1,0:T(8,128)(2,1)}, f32[16,128]{1,0:T(8,128)}, f32[8,128]{1,0:T(8,128)}) custom-call(s32[12]{0:T(128)} %lengths_ref.1, s32[16]{0:T(128)} %request_ref.1, s32[1,64]{1,0:T(1,128)} %bitcast.7, bf16[512,896]{1,0:T(8,128)(2,1)} %query_ref.1, bf16[512,1792]{1,0:T(8,128)(2,1)} %project.1.kv_ref, ...), custom_call_target="tpu_custom_call" | custom-call | tf_op jit(solution)/shard_map/attend/pallas_call | solution.py:790
  219.6 0.0 copy-start.1
  219.6 0.0 copy-start
  219.6 4.3 %copy.20 = bf16[64,8,2,896]{3,2,1,0:T(2,128)(2,1)} copy(bf16[64,8,2,896]{3,1,2,0:T(8,128)(2,1)} %bitcast.5) | data formatting | bytes 3670016
  223.8 0.0 copy-done.1
  223.8 0.6 slice_reduce_fusion
  224.5 1.2 slice_bitcast_fusion
  225.6 0.0 copy-done
  225.7 0.9 copy.22
Async XLA Ops:
  219.6 4.3 %copy-start.1 = (f32[16,128]{1,0:T(8,128)S(1)}, f32[16,128]{1,0:T(8,128)}, u32[]{:S(2)}) copy-start(f32[16,128]{1,0:T(8,128)} %get-tuple-element.10) | copy-start | bytes 24580
  219.6 6.1 %copy-start = (bf16[512,896]{1,0:T(8,128)(2,1)S(1)}, bf16[512,896]{1,0:T(8,128)(2,1)}, u32[]{:S(2)}) copy-start(bf16[512,896]{1,0:T(8,128)(2,1)} %get-tuple-element.24) | copy-start | bytes 2752516
